TPU v7x, 32 devices: a whole 2x2x4 slice. The times are simulated.
32 devices in a mesh: sec: 4 (over z), harm: 8 (over y, x, core).
Axes of the slice: x: 2, y: 2, z: 4, core: 2. Of those that a mesh axis runs over, the one named last changes fastest.
Arguments:
- displacement: bfloat16 [12, 64, 32, 48, 128], P('sec', 'harm'), may hold values from -3 to 3
- stiffness: bfloat16 [32, 1536, 1536], P('harm'), may hold values from -0.15625 to 0.15625
- contact_limit: float32 [12, 32, 48], P('sec', None, 'harm'), may hold values from 1 to 12
- pair_list: int32 [72, 3], replicated, may hold values from 0 to 31, as said below
- pair_count: int32 [4], replicated, may hold values from 3 to 18, as said below
Outputs:
- residual: bfloat16 [12, 64, 32, 48, 128], P('sec', 'harm')
Inputs may be any that keep to these rules, and one draw needn't show every extreme that they name: `pair_list`: rows of index i of sec (the aligned blocks of 18 rows) have owners among sectors i * 3 to i * 3 + 2 and partners equal to owner + 1 or owner - 1 modulo 12; rows at or past that index's pair_count are unused and hold entries in range; among used rows of one index, at most 6 have partners on the same index, at most 6 on index i + 1 and at most 6 on index i - 1 (modulo the size of sec), and some index reaches 6 in all three groups in every draw. `pair_count`: every index of sec has at least one used row in each of its three groups; some index uses all its rows.
All inputs are finite; a program needn't handle non-finite values.
Results may differ from a plain program's by a relative error of at most 0.004.
Values may be sent and summed in bfloat16 or wider, within the bound.
No kernel may reach another device: no remote copies, remote signals or barrier semaphores. Data moves between devices by JAX's collectives and lax.ppermute only.
A program may use at most 192 MiB of HBM per device.

v0:
```python
import math

import jax
import jax.numpy as jnp
from jax import lax
from jax.sharding import PartitionSpec as P

NT = 128


def with_halo(cells, sides, width):
    for axis, dim in sides:
        count = lax.axis_size(axis)
        head = lax.slice_in_dim(cells, 0, width, axis=dim)
        tail = lax.slice_in_dim(cells, cells.shape[dim] - width, cells.shape[dim], axis=dim)
        cells = jnp.concatenate(
            [
                lax.ppermute(tail, axis, [(i, (i + 1) % count) for i in range(count)]),
                cells,
                lax.ppermute(head, axis, [((i + 1) % count, i) for i in range(count)]),
            ],
            axis=dim,
        )
    return cells


def tables(sample_count, coeff_count):
    n_index = jnp.arange(sample_count, dtype=jnp.int32)[:, None]
    c_index = jnp.arange(coeff_count, dtype=jnp.int32)[None, :]
    harmonic = c_index // 2 + 1
    phases = (harmonic * n_index % sample_count).astype(jnp.float32) * (
        2.0 * math.pi / sample_count
    )
    waveform = jnp.where(c_index % 2 == 0, jnp.cos(phases), jnp.sin(phases))
    return (waveform.astype(jnp.bfloat16), (waveform * (2.0 / sample_count)).astype(jnp.bfloat16))


def on_device(displacement, stiffness, contact_limit, pair_list, pair_count):
    sec_count = lax.axis_size("sec")
    sec_index = lax.axis_index("sec")
    harm_count = lax.axis_size("harm")
    sectors_here, coeffs_here, blocks_total, dofs_total, batch_cols = displacement.shape
    coeff_total = coeffs_here * harm_count
    forward_table, inverse_table = tables(NT, coeff_total)
    exchanged = lax.all_to_all(displacement, "harm", split_axis=3, concat_axis=1, tiled=True)
    waveform = jnp.einsum(
        "nc,scbdx->snbdx", forward_table, exchanged, preferred_element_type=jnp.float32
    )
    samples = waveform.astype(jnp.bfloat16)
    slots_dev = pair_list.shape[0] // sec_count
    capacity = slots_dev // 3
    sector_total = sectors_here * sec_count

    def bucket(device):
        rows = lax.dynamic_slice_in_dim(pair_list, device * slots_dev, slots_dev, 0)
        row_index = jnp.arange(slots_dev, dtype=jnp.int32)
        is_valid = row_index < pair_count[device]
        owners = rows[:, 0]
        partners = rows[:, 1]
        blocks = rows[:, 2]
        partner_dev = partners // sectors_here
        group = jnp.where(
            partner_dev == device, 0, jnp.where(partners == (owners + 1) % sector_total, 1, 2)
        )
        matches = (
            (group[:, None] == jnp.arange(3, dtype=jnp.int32)[None, :]) & is_valid[:, None]
        ).astype(jnp.int32)
        before = jnp.cumsum(matches, axis=0) - matches
        ranking = jnp.sum(before * matches, axis=1)
        slot_index = jnp.where(is_valid, group * capacity + ranking, slots_dev)
        source = jnp.zeros((slots_dev,), jnp.int32).at[slot_index].set(row_index, mode="drop")
        live = jnp.zeros((slots_dev,), jnp.int32).at[slot_index].set(1, mode="drop")
        return (
            owners[source] - device * sectors_here,
            partners[source] - partner_dev[source] * sectors_here,
            blocks[source],
            live > 0,
        )

    own_owner, own_partner, own_block, own_live = bucket(sec_index)
    prev_bucket = bucket((sec_index + sec_count - 1) % sec_count)
    next_bucket = bucket((sec_index + 1) % sec_count)
    send_order = jnp.concatenate(
        [
            jnp.arange(2 * capacity, 3 * capacity, dtype=jnp.int32),
            jnp.arange(capacity, 2 * capacity, dtype=jnp.int32),
        ]
    )
    send_owner = own_owner[send_order]
    send_block = own_block[send_order]
    send_live = own_live[send_order]
    outgoing = samples[send_owner, :, send_block]
    outgoing = jnp.where(send_live[:, None, None, None], outgoing, jnp.zeros_like(outgoing))
    padded = with_halo(outgoing.reshape((2, capacity) + outgoing.shape[1:]), (("sec", 0),), 1)
    remote_wave = jnp.concatenate([padded[0], padded[3]], axis=0)
    local_wave = samples[own_owner[:capacity], :, own_block[:capacity]]
    owner_wave = jnp.concatenate([local_wave, remote_wave], axis=0)
    partner_index = jnp.concatenate(
        [
            own_partner[:capacity],
            prev_bucket[1][capacity : 2 * capacity],
            next_bucket[1][2 * capacity :],
        ]
    )
    block_index = jnp.concatenate(
        [
            own_block[:capacity],
            prev_bucket[2][capacity : 2 * capacity],
            next_bucket[2][2 * capacity :],
        ]
    )
    live_rows = jnp.concatenate(
        [
            own_live[:capacity],
            prev_bucket[3][capacity : 2 * capacity],
            next_bucket[3][2 * capacity :],
        ]
    )
    partner_wave = samples[partner_index, :, block_index]
    limits = contact_limit[partner_index, block_index][:, None, :, None]
    relative = owner_wave.astype(jnp.float32) - partner_wave.astype(jnp.float32)
    friction = jnp.where(
        live_rows[:, None, None, None], limits * jnp.tanh(relative / limits), jnp.float32(0.0)
    ).astype(jnp.bfloat16)
    pair_coeffs = jnp.einsum(
        "nc,rndx->rcdx", inverse_table, friction, preferred_element_type=jnp.float32
    ).astype(jnp.bfloat16)
    force = jnp.zeros(
        (sectors_here, coeff_total, blocks_total, samples.shape[3], batch_cols), jnp.float32
    )
    force = force.at[partner_index, :, block_index].add(-pair_coeffs.astype(jnp.float32))
    force = force.at[own_owner[:capacity], :, own_block[:capacity]].add(
        pair_coeffs[:capacity].astype(jnp.float32)
    )
    remote_force = friction[capacity:]
    back = with_halo(remote_force.reshape((2, capacity) + remote_force.shape[1:]), (("sec", 0),), 1)
    returned_wave = jnp.concatenate([back[3], back[0]], axis=0)
    returned = jnp.einsum(
        "nc,rndx->rcdx", inverse_table, returned_wave, preferred_element_type=jnp.float32
    ).astype(jnp.bfloat16)
    force = force.at[own_owner[capacity:], :, own_block[capacity:]].add(
        returned.astype(jnp.float32)
    )
    force_coeffs = force.astype(jnp.bfloat16)
    returned_coeffs = lax.all_to_all(force_coeffs, "harm", split_axis=1, concat_axis=3, tiled=True)
    harmonics_here = stiffness.shape[0]
    paired = displacement.reshape(
        sectors_here, harmonics_here, 2, blocks_total * dofs_total, batch_cols
    )
    product = jnp.einsum("hij,shpjx->shpix", stiffness, paired, preferred_element_type=jnp.float32)
    result = product.reshape(displacement.shape) + returned_coeffs.astype(jnp.float32)
    return result.astype(jnp.bfloat16)


def solution(mesh):
    in_specs = (
        P("sec", "harm", None, None, None),
        P("harm", None, None),
        P("sec", None, "harm"),
        P(),
        P(),
    )
    out_specs = P("sec", "harm", None, None, None)
    return jax.shard_map(
        on_device, mesh=mesh, in_specs=in_specs, out_specs=out_specs, check_vma=False
    )
```

profile of v0, /device:TPU:0, one launch (start us, length us, event | category | flops | bytes accessed | tf_op | source)
XLA Modules:
  0.0 445.3 jit_solution(13424681273661140205)
XLA Ops:
  0.0 9.9 %copy.38 = bf16[3,8,32,48,128]{4,2,1,0,3:T(8,128)(2,1)} copy(bf16[3,8,32,48,128]{4,3,2,1,0:T(8,128)(2,1)} %param.5) | data formatting | bytes 18874368 | tf_op args[0]
  9.9 5.3 %all-to-all-start = ((bf16[3,8,32,48,128]{4,2,1,0,3:T(8,128)(2,1)}), bf16[3,8,32,48,128]{4,2,1,0,3:T(8,128)(2,1)}, u32[]{:S(2)}, u32[]{:S(2)}) async-start(bf16[3,8,32,48,128]{4,2,1,0,3:T(8,128)(2,1)} %copy.38), calls=%async_computation | async-start | bytes 18874368 | tf_op jit(solution)/shard_map/all_to_all | solution.py:45
  32.7 88.4 %all-to-all-done = bf16[3,8,32,48,128]{4,2,1,0,3:T(8,128)(2,1)} async-done(((bf16[3,8,32,48,128]{4,2,1,0,3:T(8,128)(2,1)}), bf16[3,8,32,48,128]{4,2,1,0,3:T(8,128)(2,1)}, u32[]{:S(2)}, u32[]{:S(2)}) %all-to-all-start) | async-done | bytes 9437216 | tf_op jit(solution)/shard_map/all_to_all | solution.py:45
  121.1 12.1 %convert_bitcast_fusion.1 = bf16[3,128,32,6,128]{4,1,3,2,0:T(8,128)(2,1)} fusion(bf16[3,8,8,32,6,128]{5,3,2,0,4,1:T(8,128)(2,1)} %bitcast.35, s32[64]{0:T(128)S(1)} %fusion.44, pred[64]{0:T(512)(128)(4,1)S(1)} %fusion.43), kind=kOutput, calls=%fused_computation.31 | convolution fusion | flops 1217527808 | bytes 28311872 | tf_op jit(solution)/shard_map/nc,scbdx->snbdx/dot_general | solution.py:46
  133.2 7.4 %gather_fusion.15 = bf16[12,128,6,128]{3,1,2,0:T(8,128)(2,1)S(1)} fusion(bf16[3,128,32,6,128]{4,1,3,2,0:T(8,128)(2,1)} %convert_bitcast_fusion.1, s32[12]{0:T(128)S(1)} %fusion.55), kind=kCustom, calls=%fused_computation.15 | custom fusion | bytes 4718688 | tf_op jit(solution)/shard_map/gather | solution.py:92
  152.4 7.8 %gather_fusion.16 = bf16[18,128,6,128]{3,1,2,0:T(8,128)(2,1)S(1)} fusion(bf16[3,128,32,6,128]{4,1,3,2,0:T(8,128)(2,1)} %convert_bitcast_fusion.1, s32[18]{0:T(128)S(1)} %get-tuple-element.5), kind=kCustom, calls=%fused_computation.16 | custom fusion | bytes 7078032 | tf_op jit(solution)/shard_map/gather | solution.py:119
  160.2 8.2 %gather_fusion.11 = bf16[6,128,6,128]{3,1,2,0:T(8,128)(2,1)} fusion(bf16[3,128,32,6,128]{4,1,3,2,0:T(8,128)(2,1)} %convert_bitcast_fusion.1, s32[6]{0:T(128)S(1)} %get-tuple-element.26), kind=kCustom, calls=%fused_computation.11 | custom fusion | bytes 2359344 | tf_op jit(solution)/shard_map/gather | solution.py:96
  168.4 5.6 %collective-permute-done = bf16[1,6,128,6,128]{4,2,3,1,0:T(8,128)(2,1)} collective-permute-done((bf16[1,6,128,6,128]{4,2,3,1,0:T(8,128)(2,1)}, bf16[1,6,128,6,128]{4,2,3,1,0:T(8,128)(2,1)}, u32[]{:S(2)}, u32[]{:S(2)}) %collective-permute-start) | collective-permute-done | bytes 1179680 | tf_op jit(solution)/shard_map/ppermute | solution.py:18
  174.0 21.4 %collective-permute-done.1 = bf16[1,6,128,6,128]{4,2,3,1,0:T(8,128)(2,1)} collective-permute-done((bf16[1,6,128,6,128]{4,2,3,1,0:T(8,128)(2,1)}, bf16[1,6,128,6,128]{4,2,3,1,0:T(8,128)(2,1)}, u32[]{:S(2)}, u32[]{:S(2)}) %collective-permute-start.1) | collective-permute-done | bytes 1179680 | tf_op jit(solution)/shard_map/ppermute | solution.py:20
  195.4 4.0 select_convert_fusion
  205.4 8.9 %broadcast_in_dim.72 = f32[3,64,32,6,128]{4,1,3,2,0:T(8,128)} broadcast(f32[]{:T(128)} %constant.120.clone.1), dimensions={} | broadcast | bytes 18874372 | tf_op jit(solution)/shard_map/broadcast_in_dim | solution.py:128
  214.3 10.4 %scatter_fusion = f32[3,64,32,6,128]{4,1,3,2,0:T(8,128)} fusion(f32[3,64,32,6,128]{4,1,3,2,0:T(8,128)} %broadcast_in_dim.72, s32[18]{0:T(128)S(1)} %fusion.60, f32[18,64,6,128]{3,1,2,0:T(8,128)S(1)} %get-tuple-element.30), kind=kCustom, calls=%fused_computation.23 | custom fusion | flops 884736 | bytes 10616976 | tf_op jit(solution)/shard_map/scatter-add | solution.py:131
  229.5 25.1 %collective-permute-done.2 = bf16[1,6,128,6,128]{4,2,3,1,0:T(8,128)(2,1)} collective-permute-done((bf16[1,6,128,6,128]{4,2,3,1,0:T(8,128)(2,1)}, bf16[1,6,128,6,128]{4,2,3,1,0:T(8,128)(2,1)}, u32[]{:S(2)}, u32[]{:S(2)}) %collective-permute-start.2) | collective-permute-done | bytes 1179680 | tf_op jit(solution)/shard_map/ppermute | solution.py:20
  256.9 6.8 %scatter_fusion.2 = f32[3,64,32,6,128]{4,1,3,2,0:T(8,128)} fusion(f32[3,64,32,6,128]{4,1,3,2,0:T(8,128)} %scatter_fusion.1, s32[12]{0:T(128)S(1)} %fusion.56, f32[12,64,6,128]{3,1,2,0:T(8,128)S(1)} %convert_bitcast_fusion.2), kind=kCustom, calls=%fused_computation.25 | custom fusion | flops 589824 | bytes 7077984 | tf_op jit(solution)/shard_map/scatter-add | solution.py:141
  263.7 10.4 %convert_element_type.97 = bf16[3,64,32,6,128]{4,1,3,2,0:T(8,128)(2,1)} convert(f32[3,64,32,6,128]{4,1,3,2,0:T(8,128)} %scatter_fusion.2) | non-fusion elementwise | flops 4718592 | bytes 28311552 | tf_op jit(solution)/shard_map/convert_element_type | solution.py:144
  274.1 13.3 %copy.41 = bf16[3,64,32,6,128]{4,2,3,0,1:T(8,128)(2,1)} copy(bf16[3,64,32,6,128]{4,1,3,2,0:T(8,128)(2,1)} %convert_element_type.97) | data formatting | bytes 18874368 | tf_op jit(solution)/shard_map/convert_element_type | solution.py:144
  287.3 5.3 %all-to-all-start.1 = ((bf16[3,64,32,6,128]{4,2,3,0,1:T(8,128)(2,1)}), bf16[3,64,32,6,128]{4,2,3,0,1:T(8,128)(2,1)}, u32[]{:S(2)}, u32[]{:S(2)}) async-start(bf16[3,64,32,6,128]{4,2,3,0,1:T(8,128)(2,1)} %copy.41), calls=%async_computation.1 | async-start | bytes 18874368 | tf_op jit(solution)/shard_map/all_to_all | solution.py:145
  292.6 25.0 %fusion.6 = f32[3,4,2,1536,128]{3,4,2,0,1:T(8,128)} fusion(bf16[4,1536,1536]{2,1,0:T(8,128)(2,1)} %param.6, bf16[3,4,2,1536,128]{4,3,2,1,0:T(8,128)(2,1)} %bitcast.179), kind=kOutput, calls=%fused_computation.35 | convolution fusion | flops 14495514624 | bytes 47185920 | tf_op jit(solution)/shard_map/hij,shpjx->shpix/dot_general | solution.py:150
  317.6 18.6 %copy.36 = f32[3,4,2,1536,128]{4,3,2,1,0:T(8,128)} copy(f32[3,4,2,1536,128]{3,4,2,0,1:T(8,128)} %fusion.6) | data formatting | bytes 37748736 | tf_op jit(solution)/shard_map/hij,shpjx->shpix/transpose | solution.py:150
  336.2 61.7 %all-to-all-done.1 = bf16[3,64,32,6,128]{4,2,3,0,1:T(8,128)(2,1)} async-done(((bf16[3,64,32,6,128]{4,2,3,0,1:T(8,128)(2,1)}), bf16[3,64,32,6,128]{4,2,3,0,1:T(8,128)(2,1)}, u32[]{:S(2)}, u32[]{:S(2)}) %all-to-all-start.1) | async-done | bytes 9437216 | tf_op jit(solution)/shard_map/all_to_all | solution.py:145
  397.9 10.1 %copy.42 = bf16[3,64,32,6,128]{4,2,3,1,0:T(8,128)(2,1)} copy(bf16[3,64,32,6,128]{4,2,3,0,1:T(8,128)(2,1)} %all-to-all-done.1) | data formatting | bytes 18874368 | tf_op jit(solution)/shard_map/all_to_all | solution.py:145
  408.0 12.9 %convert_bitcast_fusion = f32[3,8,32,8,6,128]{5,2,4,1,3,0:T(8,128)} fusion(bf16[3,8,8,32,6,128]{5,3,4,2,1,0:T(8,128)(2,1)} %bitcast.178), kind=kLoop, calls=%fused_computation.26 | loop fusion | flops 4718592 | bytes 28311552 | tf_op jit(solution)/shard_map/convert_element_type | solution.py:151
  420.9 8.2 %copy.43 = f32[3,8,32,8,6,128]{5,2,4,3,1,0:T(8,128)S(1)} copy(f32[3,8,32,8,6,128]{5,2,4,1,3,0:T(8,128)} %convert_bitcast_fusion) | data formatting | bytes 37748736 | tf_op jit(solution)/shard_map/convert_element_type | solution.py:151
  429.1 16.0 %fusion.2 = bf16[3,8,32,48,128]{4,3,2,1,0:T(8,128)(2,1)} fusion(f32[3,8,32,48,128]{4,3,2,1,0:T(8,128)} %bitcast.176, f32[3,8,32,48,128]{4,2,3,1,0:T(8,128)S(1)} %bitcast.177), kind=kLoop, calls=%fused_computation.30 | loop fusion | flops 9437184 | bytes 47185920 | tf_op jit(solution)/shard_map/convert_element_type | solution.py:152
  (110 shorter events, 41.9 us)
Async XLA Ops:
  9.9 5.3 %copy-start.8 = (s32[4]{0:T(128)S(1)}, s32[4]{0:T(128)}, u32[]{:S(2)}) copy-start(s32[4]{0:T(128)} %param.9) | copy-start | bytes 52
  9.9 6.7 %copy-start.1 = (s32[72,3]{0,1:T(4,128)S(1)}, s32[72,3]{0,1:T(4,128)}, u32[]{:S(2)}) copy-start(s32[72,3]{0,1:T(4,128)} %param.8) | copy-start | bytes 2596
  9.9 111.2 %all-to-all-start = ((bf16[3,8,32,48,128]{4,2,1,0,3:T(8,128)(2,1)}), bf16[3,8,32,48,128]{4,2,1,0,3:T(8,128)(2,1)}, u32[]{:S(2)}, u32[]{:S(2)}) async-start(bf16[3,8,32,48,128]{4,2,1,0,3:T(8,128)(2,1)} %copy.38), calls=%async_computation | async-start | bytes 18874368 | tf_op jit(solution)/shard_map/all_to_all | solution.py:45
  32.5 88.6 %copy-start.3 = (pred[64]{0:T(512)(128)(4,1)}, pred[64]{0:T(512)(128)(4,1)S(1)}, u32[]{:S(2)}) copy-start(pred[64]{0:T(512)(128)(4,1)S(1)} %fusion.43) | copy-start | bytes 196
  32.6 88.5 %copy-start.5 = (s32[64]{0:T(128)}, s32[64]{0:T(128)S(1)}, u32[]{:S(2)}) copy-start(s32[64]{0:T(128)S(1)} %fusion.44) | copy-start | bytes 772
  140.9 7.9 %copy-start.2 = (f32[3,32,6]{1,2,0:T(8,128)S(1)}, f32[3,32,6]{1,2,0:T(8,128)}, u32[]{:S(2)}) copy-start(f32[3,32,6]{1,2,0:T(8,128)} %param.7) | copy-start | bytes 6916
  142.5 31.5 %collective-permute-start = (bf16[1,6,128,6,128]{4,2,3,1,0:T(8,128)(2,1)}, bf16[1,6,128,6,128]{4,2,3,1,0:T(8,128)(2,1)}, u32[]{:S(2)}, u32[]{:S(2)}) collective-permute-start(bf16[1,6,128,6,128]{4,2,3,1,0:T(8,128)(2,1)} %get-tuple-element.10), channel_id=1, source_target_pairs={{0,8},{8,16},{16,24},{24,0},{1,9},{9,17},{17,25},{25,1},{2,10},{10... | collective-permute-start | bytes 3538952 | tf_op jit(solution)/shard_map/ppermute | solution.py:18
  144.9 50.5 %collective-permute-start.1 = (bf16[1,6,128,6,128]{4,2,3,1,0:T(8,128)(2,1)}, bf16[1,6,128,6,128]{4,2,3,1,0:T(8,128)(2,1)}, u32[]{:S(2)}, u32[]{:S(2)}) collective-permute-start(bf16[1,6,128,6,128]{4,2,3,1,0:T(8,128)(2,1)} %get-tuple-element.11), channel_id=1, source_target_pairs={{8,0},{16,8},{24,16},{0,24},{9,1},{17,9},{25,17},{1,25},{10,2},{18... | collective-permute-start | bytes 3538952 | tf_op jit(solution)/shard_map/ppermute | solution.py:20
  199.4 3.9 copy-start.9
  199.4 3.9 copy-start.10
  199.4 3.9 copy-start.4
  199.5 3.9 copy-start.6
  201.2 53.4 %collective-permute-start.2 = (bf16[1,6,128,6,128]{4,2,3,1,0:T(8,128)(2,1)}, bf16[1,6,128,6,128]{4,2,3,1,0:T(8,128)(2,1)}, u32[]{:S(2)}, u32[]{:S(2)}) collective-permute-start(bf16[1,6,128,6,128]{4,2,3,1,0:T(8,128)(2,1)} %get-tuple-element.8), channel_id=1, source_target_pairs={{8,0},{16,8},{24,16},{0,24},{9,1},{17,9},{25,17},{1,25},{10,2},{18... | collective-permute-start | bytes 3538952 | tf_op jit(solution)/shard_map/ppermute | solution.py:20
  203.0 51.6 %collective-permute-start.3 = (bf16[1,6,128,6,128]{4,2,3,1,0:T(8,128)(2,1)}, bf16[1,6,128,6,128]{4,2,3,1,0:T(8,128)(2,1)}, u32[]{:S(2)}, u32[]{:S(2)}) collective-permute-start(bf16[1,6,128,6,128]{4,2,3,1,0:T(8,128)(2,1)} %get-tuple-element.9), channel_id=1, source_target_pairs={{0,8},{8,16},{16,24},{24,0},{1,9},{9,17},{17,25},{25,1},{2,10},{10... | collective-permute-start | bytes 3538952 | tf_op jit(solution)/shard_map/ppermute | solution.py:18
  214.3 11.6 %copy-start = (s32[6]{0:T(128)S(1)}, s32[6]{0:T(128)}, u32[]{:S(2)}) copy-start(s32[6]{0:T(128)} %get-tuple-element.25) | copy-start | bytes 76
  224.7 29.9 %copy-start.7 = (s32[64]{0:T(128)S(1)}, s32[64]{0:T(128)}, u32[]{:S(2)}) copy-start(s32[64]{0:T(128)} %copy-done.5) | copy-start | bytes 772
  287.3 110.6 %all-to-all-start.1 = ((bf16[3,64,32,6,128]{4,2,3,0,1:T(8,128)(2,1)}), bf16[3,64,32,6,128]{4,2,3,0,1:T(8,128)(2,1)}, u32[]{:S(2)}, u32[]{:S(2)}) async-start(bf16[3,64,32,6,128]{4,2,3,0,1:T(8,128)(2,1)} %copy.41), calls=%async_computation.1 | async-start | bytes 18874368 | tf_op jit(solution)/shard_map/all_to_all | solution.py:145
where the time goes:
time: 453 us; the launch traced here: 445 us
  waiting for transfers between devices  202 us (45%)
  local copies, waits for them, and re-layouts  111 us (25%)
  other arithmetic  72.3 us (16%)
  matrix products  41.4 us (9%)
  starting transfers between devices  17.5 us (4%)
    all_to_all x1, waiting for transfers between devices, on_device(): lax.all_to_all(displacement, 'harm', split_axis=3, concat_axis=1, tiled=T...  88.4 us
    all_to_all x1, waiting for transfers between devices, on_device(): lax.all_to_all(force_coeffs, 'harm', split_axis=1, concat_axis=3, tiled=T...  61.7 us
    ppermute x2, waiting for transfers between devices, with_halo(): lax.ppermute(head, axis, [((i + 1) % count, i) for i in range(count)])  46.5 us
    dot_general x1, matrix products, on_device(): jnp.einsum('hij,shpjx->shpix', stiffness, paired, preferred_element_type=...  25 us
    transpose x1, local copies, waits for them, and re-layouts, on_device(): jnp.einsum('hij,shpjx->shpix', stiffness, paired, preferred_element_type=...  18.6 us
    convert_element_type x1, other arithmetic, on_device(): return result.astype(jnp.bfloat16)  16 us
    convert_element_type x1, local copies, waits for them, and re-layouts, on_device(): force_coeffs = force.astype(jnp.bfloat16)  13.3 us
    convert_element_type x1, other arithmetic, on_device(): returned_coeffs.astype(jnp.float32)  12.9 us
  transfers between devices with their start and end apart: 6, of which 5 were waited for; matrix products, arithmetic and copies ran while one was open for 24% of the time, Pallas kernels for 0%

commit v1 on v0

v1 whole, which is shorter than its diff:
```python
import functools
import math

import jax
import jax.numpy as jnp
import numpy as np
from jax import lax
from jax.experimental import pallas as pl
from jax.experimental.pallas import tpu as pltpu
from jax.sharding import PartitionSpec as P


NT = 128
ANY = pl.BlockSpec(memory_space=pl.ANY)
SMEM = pl.BlockSpec(memory_space=pltpu.SMEM)
VMEM = pl.BlockSpec(memory_space=pltpu.VMEM)
F32 = jnp.float32
BF16 = jnp.bfloat16


def tables(sample_count, coeff_count):
    n_index = np.arange(sample_count)[:, None]
    c_index = np.arange(coeff_count)[None, :]
    phases = 2.0 * math.pi * ((c_index // 2 + 1) * n_index % sample_count) / sample_count
    wave = np.where(c_index % 2 == 0, np.cos(phases), np.sin(phases)).astype(np.float32)
    return jnp.asarray(wave, BF16), jnp.asarray(wave.T * np.float32(2.0 / sample_count), BF16)


def memory(mib):
    return pltpu.CompilerParams(vmem_limit_bytes=mib << 20)


def scan_rows(cap, sectors_here, sec_count, list_ref, count_ref, device, emit):
    slots = 3 * cap
    total = sectors_here * sec_count
    used = count_ref[device]

    def row(r, ranks):
        at = device * slots + r
        owner, partner, block = list_ref[0, at], list_ref[1, at], list_ref[2, at]
        local = partner - device * sectors_here
        here = (local >= 0) & (local < sectors_here)
        following = jnp.where(owner + 1 == total, 0, owner + 1)
        group = jnp.where(here, 0, jnp.where(partner == following, 1, 2))
        valid = r < used
        rank = jnp.where(group == 0, ranks[0], jnp.where(group == 1, ranks[1], ranks[2]))

        @pl.when(valid & (rank < cap))
        def _():
            emit(group, rank, owner, partner, block)

        return tuple(
            ranks[g] + jnp.where(valid & (group == g), 1, 0).astype(jnp.int32) for g in range(3)
        )

    lax.fori_loop(0, slots, row, (jnp.int32(0),) * 3)


def widen(value):
    return value.astype(F32).reshape(-1, value.shape[-1])


def unrolled(count):
    return next(u for u in (3, 2, 1) if count % u == 0)


def each(count, body):
    def step(k, carry):
        body(k)
        return carry

    lax.fori_loop(0, count, step, 0)


def batched(count, stage, process):
    width = unrolled(count)

    def step(i, carry):
        for u in range(width):
            stage(i * width + u, u)
        for u in range(width):
            process(i * width + u, u)
        return carry

    lax.fori_loop(0, count // width, step, 0)


def swap_rows(tmp_ref, buf, coeffs, dofs):
    peers, rows = buf.shape[0], buf.shape[1]
    share = rows // coeffs
    for h in range(peers):
        buf[h] = jnp.concatenate(
            [tmp_ref[pl.ds(h * share + d, coeffs, stride=dofs), :] for d in range(share)], axis=0
        ).astype(BF16)


def send_kernel(cap, sectors_here, sec_count, sec_ref, list_ref, count_ref, disp_ref,
                next_ref, prev_ref, own_ref, raw, buf, sem, sem_out, *tmp):
    slots = 3 * cap
    me = sec_ref[0]
    base = me * sectors_here

    def clear(i):
        own_ref[i] = 0

    each(4 * slots, clear)

    def own(group, rank, owner, partner, block):
        at = group * cap + rank
        own_ref[at] = owner - base
        own_ref[slots + at] = block
        own_ref[2 * slots + at] = 1
        own_ref[3 * slots + at] = partner - base

    scan_rows(cap, sectors_here, sec_count, list_ref, count_ref, me, own)

    def copy(k):
        at = cap + k
        source = disp_ref.at[own_ref[at], :, own_ref[slots + at]]
        return pltpu.make_async_copy(source, raw.at[k], sem.at[k])

    each(2 * cap, lambda k: copy(k).start())
    coeffs, dofs = raw.shape[1], raw.shape[2]

    def out(g, k):
        target = (next_ref, prev_ref)[g]
        return pltpu.make_async_copy(buf.at[g * cap + k], target.at[:, k], sem_out.at[g * cap + k])

    for g in range(2):

        def stage(k, u, g=g):
            copy(g * cap + k).wait()
            tmp[u][...] = widen(raw[g * cap + k])

        def process(k, u, g=g):
            swap_rows(tmp[u], buf.at[g * cap + k], coeffs, dofs)
            out(g, k).start()

        batched(cap, stage, process)
    for g in range(2):
        each(cap, lambda k, g=g: out(g, k).wait())


def find_leaders(cap, blocks, sectors_here, calls, tab_ref, lead_ref, seen):
    slots = 3 * cap
    start = 0
    for firsts in calls:

        def clear(i):
            seen[i] = -1

        each(sectors_here * blocks, clear)
        for i, first in enumerate(firsts):

            def mark(k, i=i, first=first, start=start):
                at = first + k
                j = i * cap + k
                key = tab_ref[at] * blocks + tab_ref[slots + at]
                live = tab_ref[2 * slots + at] > 0
                found = jnp.where(seen[key] < 0, j, seen[key])
                lead_ref[start + j] = jnp.where(live, found, -1)
                seen[key] = jnp.where(live, found, seen[key])

            each(cap, mark)
        start += cap * len(firsts)


def local_kernel(cap, own_ref, disp_ref, diff_ref, raw, buf, sem, sem_out, *tmp):
    slots = 3 * cap

    def copy(sec_at, blk_at, j):
        source = disp_ref.at[own_ref[sec_at], :, own_ref[blk_at]]
        return pltpu.make_async_copy(source, raw.at[j], sem.at[j])

    def owner(k):
        return copy(k, slots + k, k)

    def partner(k):
        return copy(3 * slots + k, slots + k, cap + k)

    def start(k):
        owner(k).start()
        partner(k).start()

    each(cap, start)
    coeffs, dofs = raw.shape[1], raw.shape[2]

    def out(k):
        return pltpu.make_async_copy(buf.at[k], diff_ref.at[:, k], sem_out.at[k])

    def stage(k, u):
        owner(k).wait()
        partner(k).wait()
        tmp[u][...] = widen(raw[k]) - widen(raw[cap + k])

    def process(k, u):
        swap_rows(tmp[u], buf.at[k], coeffs, dofs)
        out(k).start()

    batched(cap, stage, process)
    each(cap, lambda k: out(k).wait())


def partner_kernel(cap, sectors_here, sec_count, calls, sec_ref, list_ref, count_ref, own_ref,
                   lim_ref, disp_ref, dep_ref, a_ref, b_ref, tab_ref, lead_ref, pick_ref, raw,
                   buf, seen, sem, sem_out, *tmp):
    slots = 3 * cap
    me = sec_ref[0]
    base = me * sectors_here

    def fill(i):
        keep = lax.rem(i, slots) < cap
        tab_ref[3 * slots + i] = own_ref[i]
        first = jnp.where(i < slots, own_ref[3 * slots + lax.rem(i, slots)], own_ref[i])
        tab_ref[i] = jnp.where(keep, first, 0)

    each(3 * slots, fill)
    scan = functools.partial(scan_rows, cap, sectors_here, sec_count, list_ref, count_ref)

    def incoming(wanted):
        def emit(group, rank, owner, partner, block):
            @pl.when(group == wanted)
            def _():
                at = wanted * cap + rank
                tab_ref[at] = partner - base
                tab_ref[slots + at] = block
                tab_ref[2 * slots + at] = 1

        return emit

    scan(jnp.where(me == 0, sec_count - 1, me - 1), incoming(1))
    scan(jnp.where(me == sec_count - 1, 0, me + 1), incoming(2))

    def copy(j):
        source = disp_ref.at[tab_ref[cap + j], :, tab_ref[slots + cap + j]]
        return pltpu.make_async_copy(source, raw.at[j], sem.at[j])

    each(2 * cap, lambda j: copy(j).start())
    blocks = disp_ref.shape[2]
    find_leaders(cap, blocks, sectors_here, calls, tab_ref, lead_ref, seen)
    total = lim_ref.shape[0] // 2
    share = total // (sectors_here * blocks)

    def pick(p):
        at = (tab_ref[p] * blocks + tab_ref[slots + p]) * share
        for d in range(share):
            pick_ref[p * share + d] = lim_ref[at + d]
            pick_ref[(slots + p) * share + d] = lim_ref[total + at + d]

    each(slots, pick)
    coeffs, dofs = raw.shape[1], raw.shape[2]
    targets = (a_ref, b_ref)

    def out(g, k):
        j = g * cap + k
        return pltpu.make_async_copy(buf.at[j], targets[g].at[:, k], sem_out.at[j])

    for g in range(2):

        def stage(k, u, g=g):
            copy(g * cap + k).wait()
            tmp[u][...] = widen(raw[g * cap + k])

        def process(k, u, g=g):
            swap_rows(tmp[u], buf.at[g * cap + k], coeffs, dofs)
            out(g, k).start()

        batched(cap, stage, process)
    for g in range(2):
        each(cap, lambda k, g=g: out(g, k).wait())


def friction_pair(base, rec_base, lim_ref, fwd_ref, inv_ref, x_ref, o_ref):
    peers, rows, lanes = x_ref.shape
    coeffs = fwd_ref.shape[1] // peers
    dofs = rows // coeffs
    parts = [x_ref[h].astype(F32) for h in range(peers)]
    columns = jnp.concatenate(
        [
            jnp.concatenate([x[d * coeffs : (d + 1) * coeffs] for x in parts], axis=0)
            for d in range(dofs)
        ],
        axis=1,
    ).astype(BF16)
    wave = jnp.dot(fwd_ref[...], columns, preferred_element_type=F32)
    force = jnp.concatenate(
        [
            lim_ref[base + d]
            * jnp.tanh(wave[:, d * lanes : (d + 1) * lanes] * lim_ref[rec_base + d])
            for d in range(dofs)
        ],
        axis=1,
    ).astype(BF16)
    back = jnp.dot(inv_ref[...], force, preferred_element_type=F32)
    for h in range(peers):
        o_ref[h] = jnp.concatenate(
            [
                back[h * coeffs : (h + 1) * coeffs, d * lanes : (d + 1) * lanes]
                for d in range(dofs)
            ],
            axis=0,
        ).astype(BF16)


def difference_kernel(x_ref, y_ref, *refs):
    o_ref = refs[-1]

    def subtract(h):
        o_ref[h] = (x_ref[h].astype(F32) - y_ref[h].astype(F32)).astype(BF16)

    each(x_ref.shape[0], subtract)


def friction_kernel(cap, group, first, with_difference, lim_ref, fwd_ref, inv_ref, x_ref, *refs):
    slots = 3 * cap
    if with_difference:
        y_ref, z_ref, o_ref, x_buf, o_buf, sem, y_buf, z_buf = refs
    else:
        o_ref, x_buf, o_buf, sem = refs
    dofs = x_ref.shape[2] * x_ref.shape[0] // fwd_ref.shape[1]

    def load(k):
        return pltpu.make_async_copy(x_ref.at[:, first + k], x_buf.at[k], sem.at[0, k])

    def load_y(k):
        return pltpu.make_async_copy(y_ref.at[:, k], y_buf.at[k], sem.at[2, k])

    def load_z(k):
        return pltpu.make_async_copy(z_ref.at[:, k], z_buf.at[k], sem.at[3, k])

    def out(k):
        return pltpu.make_async_copy(o_buf.at[k], o_ref.at[:, k], sem.at[1, k])

    each(cap, lambda k: load(k).start())
    if with_difference:

        def start(k):
            load_y(k).start()
            load_z(k).start()

        each(cap, start)

    def stage(k, u):
        load(k).wait()

    def process(k, u):
        base = (group * cap + k) * dofs
        rec_base = base + slots * dofs
        friction_pair(base, rec_base, lim_ref, fwd_ref, inv_ref, x_buf.at[k], o_buf.at[k])
        out(k).start()

    batched(cap, stage, process)
    if with_difference:

        def subtract(k):
            load_y(k).wait()
            load_z(k).wait()
            o_buf[cap + k] = (y_buf[k].astype(F32) - z_buf[k].astype(F32)).astype(BF16)
            out(cap + k).start()

        each(cap, subtract)
        each(2 * cap, lambda k: out(k).wait())
    else:
        each(cap, lambda k: out(k).wait())


def add_kernel(cap, specs, start, n_deps, tab_ref, lead_ref, *refs):
    n_parts = len({spec[0] for spec in specs})
    parts = refs[:n_parts]
    refs = refs[n_parts + n_deps + 1 :]
    out_ref, acc, obuf, pbuf, sem_in, sem_part, sem_out = refs[:7]
    tmp = refs[7:]
    slots = 3 * cap
    coeffs, dofs = acc.shape[1], acc.shape[2]

    def slot(first, k):
        return out_ref.at[tab_ref[first + k], :, tab_ref[slots + first + k]]

    for i, (part, first_part, first, _) in enumerate(specs):

        def load(k, i=i, part=part, first_part=first_part, first=first):
            j = i * cap + k
            at = lead_ref[start + j]

            @pl.when(at >= 0)
            def _():
                pltpu.make_async_copy(
                    parts[part].at[:, first_part + k], pbuf.at[j], sem_part.at[j]
                ).start()

            @pl.when(at == j)
            def _():
                pltpu.make_async_copy(slot(first, k), obuf.at[j], sem_in.at[j]).start()

        each(cap, load)

    for i, (part, first_part, first, sign) in enumerate(specs):

        def stage(k, u, i=i, part=part, first_part=first_part, first=first):
            j = i * cap + k
            at = lead_ref[start + j]

            @pl.when(at >= 0)
            def _():
                pltpu.make_async_copy(
                    parts[part].at[:, first_part + k], pbuf.at[j], sem_part.at[j]
                ).wait()
                tmp[u][...] = widen(pbuf[j])

            @pl.when(at == j)
            def _():
                pltpu.make_async_copy(slot(first, k), obuf.at[j], sem_in.at[j]).wait()

        def process(k, u, i=i, sign=sign):
            j = i * cap + k
            at = lead_ref[start + j]

            def term(c):
                value = tmp[u][pl.ds(c, dofs, stride=coeffs), :]
                return value if sign > 0 else -value

            @pl.when(at == j)
            def _():
                for c in range(coeffs):
                    acc[j, c] = obuf[j, c].astype(F32) + term(c)

            @pl.when((at >= 0) & (at < j))
            def _():
                for c in range(coeffs):
                    acc[at, c] = acc[at, c] + term(c)

        batched(cap, stage, process)

    def store(first, k, j):
        return pltpu.make_async_copy(obuf.at[j], slot(first, k), sem_out.at[j])

    for i, (_, _, first, _) in enumerate(specs):

        def finish(k, i=i, first=first):
            j = i * cap + k

            @pl.when(lead_ref[start + j] == j)
            def _():
                obuf[j] = acc[j].astype(BF16)
                store(first, k, j).start()

        each(cap, finish)
    for i, (_, _, first, _) in enumerate(specs):

        def drain(k, i=i, first=first):
            j = i * cap + k

            @pl.when(lead_ref[start + j] == j)
            def _():
                store(first, k, j).wait()

        each(cap, drain)


def add_pairs(cap, specs, start, tab, lead, parts, deps, out):
    n = cap * len(specs)
    coeffs, dofs, lanes = out.shape[1], out.shape[3], out.shape[4]
    peers, rows = parts[0].shape[0], parts[0].shape[2]
    return pl.pallas_call(
        functools.partial(add_kernel, cap, specs, start, len(deps)),
        out_shape=jax.ShapeDtypeStruct(out.shape, out.dtype),
        in_specs=[SMEM, SMEM] + [ANY] * (len(parts) + len(deps) + 1),
        out_specs=ANY,
        scratch_shapes=[
            pltpu.VMEM((n, coeffs, dofs, lanes), F32),
            pltpu.VMEM((n, coeffs, dofs, lanes), BF16),
            pltpu.VMEM((n, peers, rows, lanes), BF16),
        ]
        + [pltpu.SemaphoreType.DMA((n,))] * 3
        + [pltpu.VMEM((coeffs * dofs, lanes), F32)] * unrolled(cap),
        input_output_aliases={2 + len(parts) + len(deps): 0},
        compiler_params=memory(16),
        name="add_pairs",
    )(tab, lead, *parts, *deps, out)


def stiffness_kernel(n_extra, matrix_ref, x_ref, *refs):
    out_ref = refs[n_extra]
    matrix = matrix_ref[0]
    lanes = x_ref.shape[4]
    for s in range(x_ref.shape[0]):
        rhs = jnp.concatenate([x_ref[s, 0, 0], x_ref[s, 0, 1]], axis=1)
        value = jnp.dot(matrix, rhs, preferred_element_type=F32).astype(BF16)
        for p in range(2):
            out_ref[s, 0, p] = value[:, p * lanes : (p + 1) * lanes]


def stiffness_product(stiffness, paired, first, count, out, deps):
    size = stiffness.shape[1]
    sectors, lanes = paired.shape[0], paired.shape[4]
    tile = size // 2
    extra = deps if out is None else [out] + deps
    return pl.pallas_call(
        functools.partial(stiffness_kernel, len(extra)),
        grid=(count, size // tile),
        in_specs=[
            pl.BlockSpec((1, tile, size), lambda i, j: (first + i, j, 0)),
            pl.BlockSpec((sectors, 1, 2, size, lanes), lambda i, j: (0, first + i, 0, 0, 0)),
        ]
        + [ANY] * len(extra),
        out_specs=pl.BlockSpec(
            (sectors, 1, 2, tile, lanes), lambda i, j: (0, first + i, 0, j, 0)
        ),
        out_shape=jax.ShapeDtypeStruct(paired.shape, BF16),
        input_output_aliases={} if out is None else {2: 0},
        cost_estimate=pl.CostEstimate(
            flops=4 * count * size * size * sectors * lanes,
            bytes_accessed=2 * count * size * (size + 4 * sectors * lanes),
            transcendentals=0,
        ),
        name="stiffness_product",
    )(stiffness, paired, *extra)


def on_device(displacement, stiffness, contact_limit, pair_list, pair_count):
    sec_count = lax.axis_size("sec")
    harm_count = lax.axis_size("harm")
    sectors, coeffs, blocks, dofs, lanes = displacement.shape
    harmonics = stiffness.shape[0]
    cap = pair_list.shape[0] // sec_count // 3
    slots = 3 * cap
    rows = coeffs * dofs // harm_count
    fwd, inv = tables(NT, coeffs * harm_count)
    share = (harm_count, rows, lanes)
    wire = jax.ShapeDtypeStruct((harm_count, cap, rows, lanes), BF16)
    double = jax.ShapeDtypeStruct((harm_count, 2 * cap, rows, lanes), BF16)
    sec = lax.axis_index("sec").astype(jnp.int32).reshape(1)
    listing = (sec, pair_list.T, pair_count)
    raw_slot = (coeffs, dofs, lanes)
    flats = [pltpu.VMEM((coeffs * dofs, lanes), F32)] * unrolled(cap)

    partner, owner = 0, 3 * slots
    calls = (
        (partner + cap, partner + 2 * cap, owner + cap),
        (partner, owner, owner + 2 * cap),
    )

    to_next, to_prev, own = pl.pallas_call(
        functools.partial(send_kernel, cap, sectors, sec_count),
        out_shape=[wire, wire, jax.ShapeDtypeStruct((4 * slots,), jnp.int32)],
        in_specs=[SMEM, SMEM, SMEM, ANY],
        out_specs=[ANY, ANY, SMEM],
        scratch_shapes=[
            pltpu.VMEM((2 * cap,) + raw_slot, BF16),
            pltpu.VMEM((2 * cap,) + share, BF16),
            pltpu.SemaphoreType.DMA((2 * cap,)),
            pltpu.SemaphoreType.DMA((2 * cap,)),
        ]
        + flats,
        name="send",
    )(*listing, displacement)

    forward = [(i, (i + 1) % sec_count) for i in range(sec_count)]
    backward = [((i + 1) % sec_count, i) for i in range(sec_count)]
    from_prev = lax.ppermute(to_next, "sec", forward)

    def gather(n):
        return [
            pltpu.VMEM((2 * cap,) + raw_slot, BF16),
            pltpu.VMEM((n * cap,) + share, BF16),
        ]

    diff_local = pl.pallas_call(
        functools.partial(local_kernel, cap),
        out_shape=wire,
        in_specs=[SMEM, ANY],
        out_specs=ANY,
        scratch_shapes=gather(1)
        + [pltpu.SemaphoreType.DMA((2 * cap,)), pltpu.SemaphoreType.DMA((cap,))]
        + flats,
        name="local",
    )(own, displacement)
    limit = contact_limit.reshape(-1)
    limit = jnp.concatenate([limit, 1.0 / limit])
    gathered = pl.pallas_call(
        functools.partial(partner_kernel, cap, sectors, sec_count, calls),
        out_shape=[wire] * 2
        + [jax.ShapeDtypeStruct((6 * n,), jnp.int32) for n in (slots, cap)]
        + [jax.ShapeDtypeStruct((2 * slots * contact_limit.shape[2],), F32)],
        in_specs=[SMEM] * 5 + [ANY, ANY],
        out_specs=[ANY, ANY, SMEM, SMEM, SMEM],
        scratch_shapes=gather(2)
        + [pltpu.SMEM((sectors * blocks,), jnp.int32)]
        + [pltpu.SemaphoreType.DMA((2 * cap,))] * 2
        + flats,
        name="partner",
    )(*listing, own, limit, displacement, diff_local)
    at_a, at_b, tab, lead, limits = gathered

    to_prev, from_prev, at_b = lax.optimization_barrier((to_prev, from_prev, at_b))
    from_next = lax.ppermute(to_prev, "sec", backward)


    def exchange(x):
        return lax.all_to_all(x, "harm", split_axis=0, concat_axis=0, tiled=True)

    def product(first, count, out, deps):
        return stiffness_product(stiffness, paired, first, count, out, deps)

    def friction(group, x, first, extra=()):
        n = cap * (2 if extra else 1)
        return pl.pallas_call(
            functools.partial(friction_kernel, cap, group, first, bool(extra)),
            out_shape=double if extra else wire,
            in_specs=[SMEM, VMEM, VMEM] + [ANY] * (1 + len(extra)),
            out_specs=ANY,
            scratch_shapes=[
                pltpu.VMEM((cap,) + share, BF16),
                pltpu.VMEM((n,) + share, BF16),
                pltpu.SemaphoreType.DMA((4, n)),
            ]
            + [pltpu.VMEM((cap,) + share, BF16)] * len(extra),
            compiler_params=memory(12),
            name="friction",
        )(limits, fwd, inv, x, *extra)

    paired = displacement.reshape(sectors, harmonics, 2, blocks * dofs, lanes)
    quarter = max(harmonics // 4, 1)
    third = harmonics - 2 * quarter

    local_x = exchange(diff_local)
    diff_a = pl.pallas_call(
        difference_kernel,
        out_shape=wire,
        in_specs=[VMEM, VMEM, ANY],
        out_specs=VMEM,
        compiler_params=memory(8),
        name="difference",
    )(from_prev, at_a, local_x)
    a_x = exchange(diff_a)
    out = product(0, quarter, None, [diff_a])
    middle = friction(1, a_x, 0, (from_next, at_b))
    mixed = exchange(middle)
    out = product(quarter, third, out, [middle])
    force_local = friction(0, local_x, 0)
    ret_a = lax.ppermute(mixed[:, :cap], "sec", backward)
    force_b = friction(2, mixed, cap)
    back_b = exchange(force_b)
    out = product(quarter + third, quarter, out, [force_b])
    back_b, force_local, out = lax.optimization_barrier((back_b, force_local, out))
    ret_b = lax.ppermute(back_b, "sec", forward)
    back_local = exchange(force_local)

    out = out.reshape(displacement.shape)
    out = add_pairs(
        cap,
        ((0, 0, calls[0][0], -1), (1, 0, calls[0][1], -1), (2, 0, calls[0][2], 1)),
        0,
        tab,
        lead,
        [mixed, back_b, ret_a],
        [],
        out,
    )
    return add_pairs(
        cap,
        ((0, 0, calls[1][0], -1), (0, 0, calls[1][1], 1), (1, 0, calls[1][2], 1)),
        3 * cap,
        tab,
        lead,
        [back_local, ret_b],
        [],
        out,
    )


def solution(mesh):
    in_specs = (
        P("sec", "harm", None, None, None),
        P("harm", None, None),
        P("sec", None, "harm"),
        P(),
        P(),
    )
    out_specs = P("sec", "harm", None, None, None)

    return jax.shard_map(
        on_device, mesh=mesh, in_specs=in_specs, out_specs=out_specs, check_vma=False
    )
```

time: 453 us -> 120 us (0.26); the launches traced: 445 us -> 119 us
  waiting for transfers between devices: 202 us -> 17.6 us
  local copies, waits for them, and re-layouts: 111 us -> 4.6 us
  other arithmetic: 72.3 us -> 0.68 us
  Pallas kernels: 0 us -> 59.9 us
  matrix products: 41.4 us -> 0 us
  blocking collectives: 0 us -> 13.6 us
  starting transfers between devices: 17.5 us -> 22.2 us
    all_to_all x2 -> x4, waiting for transfers between devices: 150 us -> 9.36 us  [exchange(): return lax.all_to_all(x, 'harm', split_axis=0, concat_axis=0, tiled=True)]
    pallas_call x0 -> x12, Pallas kernels: none -> 59.9 us  [the longest x3 27.1 us: stiffness_product(): pl.pallas_call(functools.partial(stiffness_kernel, len(extra)), grid=(cou...]
    convert_element_type x8 -> x0, other arithmetic: 44.6 us -> none  [the longest x1 16 us: on_device(): return result.astype(jnp.bfloat16)]
    ppermute x4, waiting for transfers between devices: 52.1 us -> 8.27 us  [the longest x1 5 us: on_device(): ret_b = lax.ppermute(back_b, 'sec', forward)]
    dot_general x4 -> x0, matrix products: 41.4 us -> none  [the longest x1 25 us: on_device(): jnp.einsum('hij,shpjx->shpix', stiffness, paired, preferred_element_type=...]
    gather x17 -> x0, local copies, waits for them, and re-layouts: 33.8 us -> none  [the longest x1 8.16 us: on_device(): local_wave = samples[own_owner[:capacity], :, own_block[:capacity]]]
    convert_element_type x2 -> x0, local copies, waits for them, and re-layouts: 21.4 us -> none  [the longest x1 13.3 us: on_device(): force_coeffs = force.astype(jnp.bfloat16)]
    scatter-add x3 -> x0, other arithmetic: 20.8 us -> none  [the longest x1 10.4 us: on_device(): force.at[partner_index, :, block_index]]
  transfers between devices with their start and end apart: 6 -> 8, of which waited for: 5 -> 6; matrix products, arithmetic and copies ran while one was open for 24% -> 1% of each run, Pallas kernels for 0% -> 38%
where the time goes in v1:
time: 120 us; the launch traced here: 119 us
  Pallas kernels  59.9 us (50%)
  starting transfers between devices  22.2 us (18%)
  waiting for transfers between devices  17.6 us (15%)
  blocking collectives  13.6 us (11%)
  local copies, waits for them, and re-layouts  4.6 us (4%)
    pallas_call x3, Pallas kernels, stiffness_product(): pl.pallas_call(functools.partial(stiffness_kernel, len(extra)), grid=(cou...  27.1 us
    all_to_all x4, starting transfers between devices, exchange(): return lax.all_to_all(x, 'harm', split_axis=0, concat_axis=0, tiled=True)  15 us
    all_to_all x1, blocking collectives, exchange(): return lax.all_to_all(x, 'harm', split_axis=0, concat_axis=0, tiled=True)  13.6 us
    pallas_call x3, Pallas kernels, friction(): pl.pallas_call(functools.partial(friction_kernel, cap, group, first, bool...  9.73 us
    all_to_all x4, waiting for transfers between devices, exchange(): return lax.all_to_all(x, 'harm', split_axis=0, concat_axis=0, tiled=True)  9.36 us
    pallas_call x2, Pallas kernels, add_pairs(): pl.pallas_call(functools.partial(add_kernel, cap, specs, start, len(deps)...  7.93 us
    pallas_call x1, Pallas kernels, on_device(): pl.pallas_call(functools.partial(partner_kernel, cap, sectors, sec_count,...  6.63 us
    ppermute x1, waiting for transfers between devices, on_device(): ret_b = lax.ppermute(back_b, 'sec', forward)  5 us
  transfers between devices with their start and end apart: 8, of which 6 were waited for; matrix products, arithmetic and copies ran while one was open for 1% of the time, Pallas kernels for 38%

profile of v1, /device:TPU:0, one launch (start us, length us, event | category | flops | bytes accessed | tf_op | source)
XLA Modules:
  0.0 118.7 jit_solution(12296399818593663704)
XLA Ops:
  0.0 4.9 %send.1 = (bf16[8,6,48,128]{3,2,1,0:T(8,128)(2,1)}, bf16[8,6,48,128]{3,2,1,0:T(8,128)(2,1)}, s32[72]{0:T(128)}) custom-call(s32[1]{0:T(128)} %bitcast.sec_ref, s32[3,72]{1,0:T(4,128)} %bitcast.8, s32[4]{0:T(128)} %count_ref.3, bf16[3,8,32,48,128]{4,3,2,1,0:T(8,128)(2,1)} %disp_ref.5), custom_call_target="tpu_custom_call" | custom-call | tf_op jit(solution)/shard_map/send/pallas_call | solution.py:543
  4.9 3.1 %collective-permute-start = (bf16[8,6,48,128]{3,2,1,0:T(8,128)(2,1)}, bf16[8,6,48,128]{3,2,1,0:T(8,128)(2,1)S(1)}, u32[]{:S(2)}, u32[]{:S(2)}) collective-permute-start(bf16[8,6,48,128]{3,2,1,0:T(8,128)(2,1)} %get-tuple-element.24), channel_id=1, source_target_pairs={{0,8},{8,16},{16,24},{24,0},{1,9},{9,17},{17,25},{25,1},{2,10},{10... | collective-permute-start | bytes 1769480 | tf_op jit(solution)/shard_map/ppermute | solution.py:560
  8.0 3.5 %local.1.dep_ref = bf16[8,6,48,128]{3,2,1,0:T(8,128)(2,1)} custom-call(s32[72]{0:T(128)} %get-tuple-element.19.own_ref, bf16[3,8,32,48,128]{4,3,2,1,0:T(8,128)(2,1)} %disp_ref.5), custom_call_target="tpu_custom_call" | custom-call | tf_op jit(solution)/shard_map/local/pallas_call | solution.py:568
  11.5 3.7 %all-to-all-start = ((bf16[8,6,48,128]{3,2,1,0:T(8,128)(2,1)}), bf16[8,6,48,128]{3,2,1,0:T(8,128)(2,1)S(1)}, u32[]{:S(2)}, u32[]{:S(2)}) async-start(bf16[8,6,48,128]{3,2,1,0:T(8,128)(2,1)} %local.1.dep_ref), calls=%async_computation | async-start | bytes 1179648 | tf_op jit(solution)/shard_map/all_to_all | solution.py:600
  16.2 6.6 %partner.1 = (bf16[8,6,48,128]{3,2,1,0:T(8,128)(2,1)}, bf16[8,6,48,128]{3,2,1,0:T(8,128)(2,1)}, s32[108]{0:T(128)}, s32[36]{0:T(128)}, f32[216]{0:T(256)}) custom-call(s32[1]{0:T(128)} %bitcast.sec_ref, s32[3,72]{1,0:T(4,128)} %bitcast.9, s32[4]{0:T(128)} %count_ref.3, s32[72]{0:T(128)} %get-tuple-element.19.own_ref, f32[1152]{0:T(1024)} %pad_maximum_fusion.lim_ref, ...), custom_call_target="tpu_custom_call" | custom-call | tf_op jit(solution)/shard_map/partner/pallas_call | solution.py:580
  23.5 1.7 %collective-permute-start.1 = (bf16[8,6,48,128]{3,2,1,0:T(8,128)(2,1)}, bf16[8,6,48,128]{3,2,1,0:T(8,128)(2,1)S(1)}, u32[]{:S(2)}, u32[]{:S(2)}) collective-permute-start(bf16[8,6,48,128]{3,2,1,0:T(8,128)(2,1)} %get-tuple-element.28), channel_id=1, source_target_pairs={{8,0},{16,8},{24,16},{0,24},{9,1},{17,9},{25,17},{1,25},{10,2},{18... | collective-permute-start | bytes 1769480 | tf_op jit(solution)/shard_map/ppermute | solution.py:596
  25.7 1.1 copy-done.2
  26.9 13.6 %all_to_all.25.x_ref = bf16[8,6,48,128]{3,2,1,0:T(8,128)(2,1)S(1)} all-to-all(bf16[8,6,48,128]{3,2,1,0:T(8,128)(2,1)S(1)} %difference.1.refs_0_), channel_id=1, replica_groups=mesh['sec'=4,'harm'=8] {'harm'}, dimensions={0} | all-to-all | bytes 1179648 | tf_op jit(solution)/shard_map/all_to_all | solution.py:600
  42.2 3.7 %friction.3.refs_1_ = bf16[8,12,48,128]{3,2,1,0:T(8,128)(2,1)} custom-call(f32[216]{0:T(256)S(1)} %copy-done.5, bf16[128,64]{1,0:T(8,128)(2,1)S(1)} %copy-done.3, bf16[64,128]{1,0:T(8,128)(2,1)S(1)} %copy-done.4, bf16[8,6,48,128]{3,2,1,0:T(8,128)(2,1)S(1)} %all_to_all.25.x_ref, bf16[8,6,48,128]{3,2,1,0:T(8,128)(2,1)S(1)} %collective-permute-done.1.refs_0_, ...), custom_call_target="tpu_custom_call" | custom-call | tf_op jit(solution)/shard_map/friction/pallas_call | solution.py:607
  45.9 3.6 %all-to-all-start.2 = ((bf16[8,12,48,128]{3,2,1,0:T(8,128)(2,1)}), bf16[8,12,48,128]{3,2,1,0:T(8,128)(2,1)S(1)}, u32[]{:S(2)}, u32[]{:S(2)}) async-start(bf16[8,12,48,128]{3,2,1,0:T(8,128)(2,1)} %friction.3.refs_1_), calls=%async_computation.2 | async-start | bytes 2359296 | tf_op jit(solution)/shard_map/all_to_all | solution.py:600
  50.2 3.0 %friction.5 = bf16[8,6,48,128]{3,2,1,0:T(8,128)(2,1)} custom-call(f32[216]{0:T(256)S(1)} %copy-done.6, bf16[128,64]{1,0:T(8,128)(2,1)S(1)} %copy-done.3, bf16[64,128]{1,0:T(8,128)(2,1)S(1)} %copy-done.4, bf16[8,6,48,128]{3,2,1,0:T(8,128)(2,1)S(1)} %all-to-all-done.refs_0_.x_ref), custom_call_target="tpu_custom_call" | custom-call | tf_op jit(solution)/shard_map/friction/pallas_call | solution.py:607
  53.2 7.4 %stiffness_product.3.refs_0_ = bf16[3,4,2,1536,128]{4,3,2,1,0:T(8,128)(2,1)} custom-call(bf16[4,1536,1536]{2,1,0:T(8,128)(2,1)} %matrix_ref.5, bf16[3,4,2,1536,128]{4,3,2,1,0:T(8,128)(2,1)} %bitcast.4, bf16[8,6,48,128]{3,2,1,0:T(8,128)(2,1)} %copy-done), custom_call_target="tpu_custom_call" | custom-call | flops 3623878656 | bytes 9437184 | tf_op jit(solution)/shard_map/stiffness_product/pallas_call | solution.py:498
  60.6 5.6 %all-to-all-done.2.x_ref.refs_0_ = bf16[8,12,48,128]{3,2,1,0:T(8,128)(2,1)S(1)} async-done(((bf16[8,12,48,128]{3,2,1,0:T(8,128)(2,1)}), bf16[8,12,48,128]{3,2,1,0:T(8,128)(2,1)S(1)}, u32[]{:S(2)}, u32[]{:S(2)}) %all-to-all-start.2) | async-done | bytes 1179680 | tf_op jit(solution)/shard_map/all_to_all | solution.py:600
  66.2 3.0 %friction.4.refs_1_ = bf16[8,6,48,128]{3,2,1,0:T(8,128)(2,1)} custom-call(f32[216]{0:T(256)S(1)} %copy-done.6, bf16[128,64]{1,0:T(8,128)(2,1)S(1)} %copy-done.3, bf16[64,128]{1,0:T(8,128)(2,1)S(1)} %copy-done.4, bf16[8,12,48,128]{3,2,1,0:T(8,128)(2,1)S(1)} %all-to-all-done.2.x_ref.refs_0_), custom_call_target="tpu_custom_call" | custom-call | tf_op jit(solution)/shard_map/friction/pallas_call | solution.py:607
  69.3 3.5 %all-to-all-start.3 = ((bf16[8,6,48,128]{3,2,1,0:T(8,128)(2,1)}), bf16[8,6,48,128]{3,2,1,0:T(8,128)(2,1)S(1)}, u32[]{:S(2)}, u32[]{:S(2)}) async-start(bf16[8,6,48,128]{3,2,1,0:T(8,128)(2,1)} %friction.4.refs_1_), calls=%async_computation.3 | async-start | bytes 1179648 | tf_op jit(solution)/shard_map/all_to_all | solution.py:600
  72.8 12.3 %stiffness_product.4.refs_0_ = bf16[3,4,2,1536,128]{4,3,2,1,0:T(8,128)(2,1)} custom-call(bf16[4,1536,1536]{2,1,0:T(8,128)(2,1)} %matrix_ref.5, bf16[3,4,2,1536,128]{4,3,2,1,0:T(8,128)(2,1)} %bitcast.5, bf16[3,4,2,1536,128]{4,3,2,1,0:T(8,128)(2,1)} %stiffness_product.3.refs_0_, bf16[8,12,48,128]{3,2,1,0:T(8,128)(2,1)} %friction.3.refs_1_), custom_call_target="tpu_custom_call", output_to_operand_aliasing={{}: (2, {})} | custom-call | flops 7247757312 | bytes 18874368 | tf_op jit(solution)/shard_map/stiffness_product/pallas_call | solution.py:498
  85.9 2.4 %collective-permute-start.3 = (bf16[8,6,48,128]{3,2,1,0:T(8,128)(2,1)}, bf16[8,6,48,128]{3,2,1,0:T(8,128)(2,1)S(1)}, u32[]{:S(2)}, u32[]{:S(2)}) collective-permute-start(bf16[8,6,48,128]{3,2,1,0:T(8,128)(2,1)} %slice.4), channel_id=1, source_target_pairs={{8,0},{16,8},{24,16},{0,24},{9,1},{17,9},{25,17},{1,25},{10,2},{18... | collective-permute-start | bytes 1769480 | tf_op jit(solution)/shard_map/ppermute | solution.py:641
  88.3 7.4 %stiffness_product.5 = bf16[3,4,2,1536,128]{4,3,2,1,0:T(8,128)(2,1)} custom-call(bf16[4,1536,1536]{2,1,0:T(8,128)(2,1)} %matrix_ref.5, bf16[3,4,2,1536,128]{4,3,2,1,0:T(8,128)(2,1)} %bitcast.6, bf16[3,4,2,1536,128]{4,3,2,1,0:T(8,128)(2,1)} %stiffness_product.4.refs_0_, bf16[8,6,48,128]{3,2,1,0:T(8,128)(2,1)} %friction.4.refs_1_), custom_call_target="tpu_custom_call", output_to_operand_aliasing={{}: (2, {})} | custom-call | flops 3623878656 | bytes 9437184 | tf_op jit(solution)/shard_map/stiffness_product/pallas_call | solution.py:498
  95.7 4.1 %all-to-all-start.4 = ((bf16[8,6,48,128]{3,2,1,0:T(8,128)(2,1)}), bf16[8,6,48,128]{3,2,1,0:T(8,128)(2,1)S(1)}, u32[]{:S(2)}, u32[]{:S(2)}) async-start(bf16[8,6,48,128]{3,2,1,0:T(8,128)(2,1)} %friction.5), calls=%async_computation.4 | async-start | bytes 1179648 | tf_op jit(solution)/shard_map/all_to_all | solution.py:600
  99.8 2.5 %collective-permute-done.3.refs_2_ = bf16[8,6,48,128]{3,2,1,0:T(8,128)(2,1)S(1)} collective-permute-done((bf16[8,6,48,128]{3,2,1,0:T(8,128)(2,1)}, bf16[8,6,48,128]{3,2,1,0:T(8,128)(2,1)S(1)}, u32[]{:S(2)}, u32[]{:S(2)}) %collective-permute-start.3) | collective-permute-done | bytes 589856 | tf_op jit(solution)/shard_map/ppermute | solution.py:641
  102.4 4.5 %add_pairs.2.refs_2_ = bf16[3,8,32,48,128]{4,3,2,1,0:T(8,128)(2,1)} custom-call(s32[108]{0:T(128)S(1)} %copy-done.7, s32[36]{0:T(128)S(1)} %copy-done.8, bf16[8,12,48,128]{3,2,1,0:T(8,128)(2,1)S(1)} %all-to-all-done.2.x_ref.refs_0_, bf16[8,6,48,128]{3,2,1,0:T(8,128)(2,1)S(1)} %all-to-all-done.3.refs_1_, ...), custom_call_target="tpu_custom_call", output_to_operand_aliasing={{}: (5, {})} | custom-call | tf_op jit(solution)/shard_map/add_pairs/pallas_call | solution.py:464
  106.9 3.4 %all-to-all-done.4.refs_0_ = bf16[8,6,48,128]{3,2,1,0:T(8,128)(2,1)S(1)} async-done(((bf16[8,6,48,128]{3,2,1,0:T(8,128)(2,1)}), bf16[8,6,48,128]{3,2,1,0:T(8,128)(2,1)S(1)}, u32[]{:S(2)}, u32[]{:S(2)}) %all-to-all-start.4) | async-done | bytes 589856 | tf_op jit(solution)/shard_map/all_to_all | solution.py:600
  110.3 5.0 %collective-permute-done.2.refs_1_ = bf16[8,6,48,128]{3,2,1,0:T(8,128)(2,1)S(1)} collective-permute-done((bf16[8,6,48,128]{3,2,1,0:T(8,128)(2,1)S(1)}, bf16[8,6,48,128]{3,2,1,0:T(8,128)(2,1)S(1)}, u32[]{:S(2)}, u32[]{:S(2)}) %collective-permute-start.2) | collective-permute-done | bytes 589856 | tf_op jit(solution)/shard_map/ppermute | solution.py:646
  115.3 3.5 %add_pairs.3 = bf16[3,8,32,48,128]{4,3,2,1,0:T(8,128)(2,1)} custom-call(s32[108]{0:T(128)S(1)} %copy-done.7, s32[36]{0:T(128)S(1)} %copy-done.8, bf16[8,6,48,128]{3,2,1,0:T(8,128)(2,1)S(1)} %all-to-all-done.4.refs_0_, bf16[8,6,48,128]{3,2,1,0:T(8,128)(2,1)S(1)} %collective-permute-done.2.refs_1_, ...), custom_call_target="tpu_custom_call", output_to_operand_aliasing={{}: (4, {})} | custom-call | tf_op jit(solution)/shard_map/add_pairs/pallas_call | solution.py:464
  (30 shorter events, 5.5 us)
Async XLA Ops:
  0.0 15.2 %copy-start.9 = (f32[3,32,6]{1,2,0:T(8,128)S(1)}, f32[3,32,6]{1,2,0:T(8,128)}, u32[]{:S(2)}) copy-start(f32[3,32,6]{1,2,0:T(8,128)} %param.9) | copy-start | bytes 6916
  4.9 18.7 %collective-permute-start = (bf16[8,6,48,128]{3,2,1,0:T(8,128)(2,1)}, bf16[8,6,48,128]{3,2,1,0:T(8,128)(2,1)S(1)}, u32[]{:S(2)}, u32[]{:S(2)}) collective-permute-start(bf16[8,6,48,128]{3,2,1,0:T(8,128)(2,1)} %get-tuple-element.24), channel_id=1, source_target_pairs={{0,8},{8,16},{16,24},{24,0},{1,9},{9,17},{17,25},{25,1},{2,10},{10... | collective-permute-start | bytes 1769480 | tf_op jit(solution)/shard_map/ppermute | solution.py:560
  11.5 29.0 %copy-start.3 = (bf16[128,64]{1,0:T(8,128)(2,1)S(1)}, bf16[128,64]{1,0:T(8,128)(2,1)}, u32[]{:S(2)}) copy-start(bf16[128,64]{1,0:T(8,128)(2,1)} %constant.11.clone.fwd_ref) | copy-start | bytes 49156
  11.5 29.0 %copy-start.4 = (bf16[64,128]{1,0:T(8,128)(2,1)S(1)}, bf16[64,128]{1,0:T(8,128)(2,1)}, u32[]{:S(2)}) copy-start(bf16[64,128]{1,0:T(8,128)(2,1)} %constant.12.clone.inv_ref) | copy-start | bytes 49156
  11.5 14.1 %all-to-all-start = ((bf16[8,6,48,128]{3,2,1,0:T(8,128)(2,1)}), bf16[8,6,48,128]{3,2,1,0:T(8,128)(2,1)S(1)}, u32[]{:S(2)}, u32[]{:S(2)}) async-start(bf16[8,6,48,128]{3,2,1,0:T(8,128)(2,1)} %local.1.dep_ref), calls=%async_computation | async-start | bytes 1179648 | tf_op jit(solution)/shard_map/all_to_all | solution.py:600
  23.5 16.9 %collective-permute-start.1 = (bf16[8,6,48,128]{3,2,1,0:T(8,128)(2,1)}, bf16[8,6,48,128]{3,2,1,0:T(8,128)(2,1)S(1)}, u32[]{:S(2)}, u32[]{:S(2)}) collective-permute-start(bf16[8,6,48,128]{3,2,1,0:T(8,128)(2,1)} %get-tuple-element.28), channel_id=1, source_target_pairs={{8,0},{16,8},{24,16},{0,24},{9,1},{17,9},{25,17},{1,25},{10,2},{18... | collective-permute-start | bytes 1769480 | tf_op jit(solution)/shard_map/ppermute | solution.py:596
  25.7 1.1 copy-start.2
  26.9 26.3 %copy-start = (bf16[8,6,48,128]{3,2,1,0:T(8,128)(2,1)}, bf16[8,6,48,128]{3,2,1,0:T(8,128)(2,1)S(1)}, u32[]{:S(2)}) copy-start(bf16[8,6,48,128]{3,2,1,0:T(8,128)(2,1)S(1)} %difference.1.refs_0_) | copy-start | bytes 1769476
  40.5 1.1 copy-start.1
  41.5 0.7 copy-start.5
  45.9 20.3 %all-to-all-start.2 = ((bf16[8,12,48,128]{3,2,1,0:T(8,128)(2,1)}), bf16[8,12,48,128]{3,2,1,0:T(8,128)(2,1)S(1)}, u32[]{:S(2)}, u32[]{:S(2)}) async-start(bf16[8,12,48,128]{3,2,1,0:T(8,128)(2,1)} %friction.3.refs_1_), calls=%async_computation.2 | async-start | bytes 2359296 | tf_op jit(solution)/shard_map/all_to_all | solution.py:600
  49.5 0.7 copy-start.6
  69.3 26.5 %all-to-all-start.3 = ((bf16[8,6,48,128]{3,2,1,0:T(8,128)(2,1)}), bf16[8,6,48,128]{3,2,1,0:T(8,128)(2,1)S(1)}, u32[]{:S(2)}, u32[]{:S(2)}) async-start(bf16[8,6,48,128]{3,2,1,0:T(8,128)(2,1)} %friction.4.refs_1_), calls=%async_computation.3 | async-start | bytes 1179648 | tf_op jit(solution)/shard_map/all_to_all | solution.py:600
  85.9 16.4 %copy-start.7 = (s32[108]{0:T(128)S(1)}, s32[108]{0:T(128)}, u32[]{:S(2)}) copy-start(s32[108]{0:T(128)} %get-tuple-element.20.tab_ref) | copy-start | bytes 1300
  85.9 16.4 %copy-start.8 = (s32[36]{0:T(128)S(1)}, s32[36]{0:T(128)}, u32[]{:S(2)}) copy-start(s32[36]{0:T(128)} %get-tuple-element.21.lead_ref) | copy-start | bytes 436
  85.9 16.4 %collective-permute-start.3 = (bf16[8,6,48,128]{3,2,1,0:T(8,128)(2,1)}, bf16[8,6,48,128]{3,2,1,0:T(8,128)(2,1)S(1)}, u32[]{:S(2)}, u32[]{:S(2)}) collective-permute-start(bf16[8,6,48,128]{3,2,1,0:T(8,128)(2,1)} %slice.4), channel_id=1, source_target_pairs={{8,0},{16,8},{24,16},{0,24},{9,1},{17,9},{25,17},{1,25},{10,2},{18... | collective-permute-start | bytes 1769480 | tf_op jit(solution)/shard_map/ppermute | solution.py:641
  95.7 19.5 %collective-permute-start.2 = (bf16[8,6,48,128]{3,2,1,0:T(8,128)(2,1)S(1)}, bf16[8,6,48,128]{3,2,1,0:T(8,128)(2,1)S(1)}, u32[]{:S(2)}, u32[]{:S(2)}) collective-permute-start(bf16[8,6,48,128]{3,2,1,0:T(8,128)(2,1)S(1)} %all-to-all-done.3.refs_1_), channel_id=1, source_target_pairs={{0,8},{8,16},{16,24},{24,0},{1,9},{9,17},{17,25},{25,1},{2,10},{10... | collective-permute-start | bytes 1769480 | tf_op jit(solution)/shard_map/ppermute | solution.py:646
  95.7 14.5 %all-to-all-start.4 = ((bf16[8,6,48,128]{3,2,1,0:T(8,128)(2,1)}), bf16[8,6,48,128]{3,2,1,0:T(8,128)(2,1)S(1)}, u32[]{:S(2)}, u32[]{:S(2)}) async-start(bf16[8,6,48,128]{3,2,1,0:T(8,128)(2,1)} %friction.5), calls=%async_computation.4 | async-start | bytes 1179648 | tf_op jit(solution)/shard_map/all_to_all | solution.py:600

commit v2 on v1

--- a/solution.py
+++ b/solution.py
@@ -95,50 +95,66 @@
 
 
 def send_kernel(cap, sectors_here, sec_count, sec_ref, list_ref, count_ref, disp_ref,
-                next_ref, prev_ref, own_ref, raw, buf, sem, sem_out, *tmp):
+                next_ref, tab_ref, raw, buf, sem, sem_out, *tmp):
     slots = 3 * cap
     me = sec_ref[0]
     base = me * sectors_here
+    scan = functools.partial(scan_rows, cap, sectors_here, sec_count, list_ref, count_ref)
 
     def clear(i):
-        own_ref[i] = 0
-
-    each(4 * slots, clear)
+        tab_ref[i] = 0
+
+    each(6 * slots, clear)
 
     def own(group, rank, owner, partner, block):
         at = group * cap + rank
-        own_ref[at] = owner - base
-        own_ref[slots + at] = block
-        own_ref[2 * slots + at] = 1
-        own_ref[3 * slots + at] = partner - base
-
-    scan_rows(cap, sectors_here, sec_count, list_ref, count_ref, me, own)
+        tab_ref[3 * slots + at] = owner - base
+        tab_ref[4 * slots + at] = block
+        tab_ref[5 * slots + at] = 1
+
+        @pl.when(group == 0)
+        def _():
+            tab_ref[at] = partner - base
+            tab_ref[slots + at] = block
+            tab_ref[2 * slots + at] = 1
+
+    scan(me, own)
 
     def copy(k):
-        at = cap + k
-        source = disp_ref.at[own_ref[at], :, own_ref[slots + at]]
+        at = 3 * slots + cap + k
+        source = disp_ref.at[tab_ref[at], :, tab_ref[slots + at]]
         return pltpu.make_async_copy(source, raw.at[k], sem.at[k])
 
-    each(2 * cap, lambda k: copy(k).start())
+    each(cap, lambda k: copy(k).start())
+
+    def incoming(wanted):
+        def emit(group, rank, owner, partner, block):
+            @pl.when(group == wanted)
+            def _():
+                at = wanted * cap + rank
+                tab_ref[at] = partner - base
+                tab_ref[slots + at] = block
+                tab_ref[2 * slots + at] = 1
+
+        return emit
+
+    scan(jnp.where(me == 0, sec_count - 1, me - 1), incoming(1))
+    scan(jnp.where(me == sec_count - 1, 0, me + 1), incoming(2))
     coeffs, dofs = raw.shape[1], raw.shape[2]
 
-    def out(g, k):
-        target = (next_ref, prev_ref)[g]
-        return pltpu.make_async_copy(buf.at[g * cap + k], target.at[:, k], sem_out.at[g * cap + k])
-
-    for g in range(2):
-
-        def stage(k, u, g=g):
-            copy(g * cap + k).wait()
-            tmp[u][...] = widen(raw[g * cap + k])
-
-        def process(k, u, g=g):
-            swap_rows(tmp[u], buf.at[g * cap + k], coeffs, dofs)
-            out(g, k).start()
-
-        batched(cap, stage, process)
-    for g in range(2):
-        each(cap, lambda k, g=g: out(g, k).wait())
+    def out(k):
+        return pltpu.make_async_copy(buf.at[k], next_ref.at[:, k], sem_out.at[k])
+
+    def stage(k, u):
+        copy(k).wait()
+        tmp[u][...] = widen(raw[k])
+
+    def process(k, u):
+        swap_rows(tmp[u], buf.at[k], coeffs, dofs)
+        out(k).start()
+
+    batched(cap, stage, process)
+    each(cap, lambda k: out(k).wait())
 
 
 def find_leaders(cap, blocks, sectors_here, calls, tab_ref, lead_ref, seen):
@@ -165,18 +181,18 @@
         start += cap * len(firsts)
 
 
-def local_kernel(cap, own_ref, disp_ref, diff_ref, raw, buf, sem, sem_out, *tmp):
+def local_kernel(cap, tab_ref, disp_ref, diff_ref, raw, buf, sem, sem_out, *tmp):
     slots = 3 * cap
 
     def copy(sec_at, blk_at, j):
-        source = disp_ref.at[own_ref[sec_at], :, own_ref[blk_at]]
+        source = disp_ref.at[tab_ref[sec_at], :, tab_ref[blk_at]]
         return pltpu.make_async_copy(source, raw.at[j], sem.at[j])
 
     def owner(k):
-        return copy(k, slots + k, k)
+        return copy(3 * slots + k, 4 * slots + k, k)
 
     def partner(k):
-        return copy(3 * slots + k, slots + k, cap + k)
+        return copy(k, slots + k, cap + k)
 
     def start(k):
         owner(k).start()
@@ -201,41 +217,19 @@
     each(cap, lambda k: out(k).wait())
 
 
-def partner_kernel(cap, sectors_here, sec_count, calls, sec_ref, list_ref, count_ref, own_ref,
-                   lim_ref, disp_ref, dep_ref, a_ref, b_ref, tab_ref, lead_ref, pick_ref, raw,
-                   buf, seen, sem, sem_out, *tmp):
-    slots = 3 * cap
-    me = sec_ref[0]
-    base = me * sectors_here
-
-    def fill(i):
-        keep = lax.rem(i, slots) < cap
-        tab_ref[3 * slots + i] = own_ref[i]
-        first = jnp.where(i < slots, own_ref[3 * slots + lax.rem(i, slots)], own_ref[i])
-        tab_ref[i] = jnp.where(keep, first, 0)
-
-    each(3 * slots, fill)
-    scan = functools.partial(scan_rows, cap, sectors_here, sec_count, list_ref, count_ref)
-
-    def incoming(wanted):
-        def emit(group, rank, owner, partner, block):
-            @pl.when(group == wanted)
-            def _():
-                at = wanted * cap + rank
-                tab_ref[at] = partner - base
-                tab_ref[slots + at] = block
-                tab_ref[2 * slots + at] = 1
-
-        return emit
-
-    scan(jnp.where(me == 0, sec_count - 1, me - 1), incoming(1))
-    scan(jnp.where(me == sec_count - 1, 0, me + 1), incoming(2))
-
-    def copy(j):
-        source = disp_ref.at[tab_ref[cap + j], :, tab_ref[slots + cap + j]]
-        return pltpu.make_async_copy(source, raw.at[j], sem.at[j])
-
-    each(2 * cap, lambda j: copy(j).start())
+def partner_kernel(cap, sectors_here, calls, tab_ref, lim_ref, disp_ref, dep_ref,
+                   a_ref, prev_ref, b_ref, lead_ref, pick_ref, raw, buf, seen, sem, sem_out,
+                   *tmp):
+    slots = 3 * cap
+    groups = ((cap, a_ref), (3 * slots + 2 * cap, prev_ref), (2 * cap, b_ref))
+
+    def copy(g, k):
+        at = groups[g][0] + k
+        source = disp_ref.at[tab_ref[at], :, tab_ref[slots + at]]
+        return pltpu.make_async_copy(source, raw.at[g * cap + k], sem.at[g * cap + k])
+
+    for g in range(3):
+        each(cap, lambda k, g=g: copy(g, k).start())
     blocks = disp_ref.shape[2]
     find_leaders(cap, blocks, sectors_here, calls, tab_ref, lead_ref, seen)
     total = lim_ref.shape[0] // 2
@@ -249,16 +243,15 @@
 
     each(slots, pick)
     coeffs, dofs = raw.shape[1], raw.shape[2]
-    targets = (a_ref, b_ref)
 
     def out(g, k):
         j = g * cap + k
-        return pltpu.make_async_copy(buf.at[j], targets[g].at[:, k], sem_out.at[j])
-
-    for g in range(2):
+        return pltpu.make_async_copy(buf.at[j], groups[g][1].at[:, k], sem_out.at[j])
+
+    for g in range(3):
 
         def stage(k, u, g=g):
-            copy(g * cap + k).wait()
+            copy(g, k).wait()
             tmp[u][...] = widen(raw[g * cap + k])
 
         def process(k, u, g=g):
@@ -266,7 +259,7 @@
             out(g, k).start()
 
         batched(cap, stage, process)
-    for g in range(2):
+    for g in range(3):
         each(cap, lambda k, g=g: out(g, k).wait())
 
 
@@ -314,81 +307,52 @@
 def friction_kernel(cap, group, first, with_difference, lim_ref, fwd_ref, inv_ref, x_ref, *refs):
     slots = 3 * cap
     if with_difference:
-        y_ref, z_ref, o_ref, x_buf, o_buf, sem, y_buf, z_buf = refs
+        y_ref, z_ref, o_ref, o_buf, sem = refs
     else:
-        o_ref, x_buf, o_buf, sem = refs
+        o_ref, o_buf, sem = refs
     dofs = x_ref.shape[2] * x_ref.shape[0] // fwd_ref.shape[1]
 
-    def load(k):
-        return pltpu.make_async_copy(x_ref.at[:, first + k], x_buf.at[k], sem.at[0, k])
-
-    def load_y(k):
-        return pltpu.make_async_copy(y_ref.at[:, k], y_buf.at[k], sem.at[2, k])
-
-    def load_z(k):
-        return pltpu.make_async_copy(z_ref.at[:, k], z_buf.at[k], sem.at[3, k])
-
     def out(k):
-        return pltpu.make_async_copy(o_buf.at[k], o_ref.at[:, k], sem.at[1, k])
-
-    each(cap, lambda k: load(k).start())
+        return pltpu.make_async_copy(o_buf.at[k], o_ref.at[:, k], sem.at[k])
+
     if with_difference:
 
-        def start(k):
-            load_y(k).start()
-            load_z(k).start()
-
-        each(cap, start)
-
-    def stage(k, u):
-        load(k).wait()
+        def subtract(k):
+            for h in range(x_ref.shape[0]):
+                value = y_ref[h, k].astype(F32) - z_ref[h, k].astype(F32)
+                o_buf[cap + k, h] = value.astype(BF16)
+            out(cap + k).start()
+
+        each(cap, subtract)
 
     def process(k, u):
         base = (group * cap + k) * dofs
         rec_base = base + slots * dofs
-        friction_pair(base, rec_base, lim_ref, fwd_ref, inv_ref, x_buf.at[k], o_buf.at[k])
+        friction_pair(base, rec_base, lim_ref, fwd_ref, inv_ref, x_ref.at[:, first + k], o_buf.at[k])
         out(k).start()
 
-    batched(cap, stage, process)
-    if with_difference:
-
-        def subtract(k):
-            load_y(k).wait()
-            load_z(k).wait()
-            o_buf[cap + k] = (y_buf[k].astype(F32) - z_buf[k].astype(F32)).astype(BF16)
-            out(cap + k).start()
-
-        each(cap, subtract)
-        each(2 * cap, lambda k: out(k).wait())
-    else:
-        each(cap, lambda k: out(k).wait())
+    batched(cap, lambda k, u: None, process)
+    each(o_ref.shape[1], lambda k: out(k).wait())
 
 
 def add_kernel(cap, specs, start, n_deps, tab_ref, lead_ref, *refs):
     n_parts = len({spec[0] for spec in specs})
     parts = refs[:n_parts]
     refs = refs[n_parts + n_deps + 1 :]
-    out_ref, acc, obuf, pbuf, sem_in, sem_part, sem_out = refs[:7]
-    tmp = refs[7:]
+    out_ref, acc, obuf, sem_in, sem_out = refs[:5]
+    tmp = refs[5:]
     slots = 3 * cap
     coeffs, dofs = acc.shape[1], acc.shape[2]
 
     def slot(first, k):
         return out_ref.at[tab_ref[first + k], :, tab_ref[slots + first + k]]
 
-    for i, (part, first_part, first, _) in enumerate(specs):
-
-        def load(k, i=i, part=part, first_part=first_part, first=first):
+    for i, (_, _, first, _) in enumerate(specs):
+
+        def load(k, i=i, first=first):
             j = i * cap + k
-            at = lead_ref[start + j]
-
-            @pl.when(at >= 0)
-            def _():
-                pltpu.make_async_copy(
-                    parts[part].at[:, first_part + k], pbuf.at[j], sem_part.at[j]
-                ).start()
-
-            @pl.when(at == j)
+
+            @pl.when(lead_ref[start + j] == j)
             def _():
                 pltpu.make_async_copy(slot(first, k), obuf.at[j], sem_in.at[j]).start()
 
@@ -396,18 +360,13 @@
 
     for i, (part, first_part, first, sign) in enumerate(specs):
 
-        def stage(k, u, i=i, part=part, first_part=first_part, first=first):
+        def stage(k, u, i=i, ref=parts[part], first_part=first_part, first=first):
             j = i * cap + k
-            at = lead_ref[start + j]
-
-            @pl.when(at >= 0)
-            def _():
-                pltpu.make_async_copy(
-                    parts[part].at[:, first_part + k], pbuf.at[j], sem_part.at[j]
-                ).wait()
-                tmp[u][...] = widen(pbuf[j])
-
-            @pl.when(at == j)
+            rows = ref.shape[2]
+            for h in range(ref.shape[0]):
+                tmp[u][pl.ds(h * rows, rows), :] = ref[h, first_part + k].astype(F32)
+
+            @pl.when(lead_ref[start + j] == j)
             def _():
                 pltpu.make_async_copy(slot(first, k), obuf.at[j], sem_in.at[j]).wait()
 
@@ -460,18 +419,16 @@
 def add_pairs(cap, specs, start, tab, lead, parts, deps, out):
     n = cap * len(specs)
     coeffs, dofs, lanes = out.shape[1], out.shape[3], out.shape[4]
-    peers, rows = parts[0].shape[0], parts[0].shape[2]
     return pl.pallas_call(
         functools.partial(add_kernel, cap, specs, start, len(deps)),
         out_shape=jax.ShapeDtypeStruct(out.shape, out.dtype),
-        in_specs=[SMEM, SMEM] + [ANY] * (len(parts) + len(deps) + 1),
+        in_specs=[SMEM, SMEM] + [VMEM] * len(parts) + [ANY] * (len(deps) + 1),
         out_specs=ANY,
         scratch_shapes=[
             pltpu.VMEM((n, coeffs, dofs, lanes), F32),
             pltpu.VMEM((n, coeffs, dofs, lanes), BF16),
-            pltpu.VMEM((n, peers, rows, lanes), BF16),
         ]
-        + [pltpu.SemaphoreType.DMA((n,))] * 3
+        + [pltpu.SemaphoreType.DMA((n,))] * 2
         + [pltpu.VMEM((coeffs * dofs, lanes), F32)] * unrolled(cap),
         input_output_aliases={2 + len(parts) + len(deps): 0},
         compiler_params=memory(16),
@@ -530,7 +487,6 @@
     wire = jax.ShapeDtypeStruct((harm_count, cap, rows, lanes), BF16)
     double = jax.ShapeDtypeStruct((harm_count, 2 * cap, rows, lanes), BF16)
     sec = lax.axis_index("sec").astype(jnp.int32).reshape(1)
-    listing = (sec, pair_list.T, pair_count)
     raw_slot = (coeffs, dofs, lanes)
     flats = [pltpu.VMEM((coeffs * dofs, lanes), F32)] * unrolled(cap)
 
@@ -540,61 +496,53 @@
         (partner, owner, owner + 2 * cap),
     )
 
-    to_next, to_prev, own = pl.pallas_call(
+    def gather(n_in, n_out):
+        return [
+            pltpu.VMEM((n_in * cap,) + raw_slot, BF16),
+            pltpu.VMEM((n_out * cap,) + share, BF16),
+        ]
+
+    def semaphores(n_in, n_out):
+        return [pltpu.SemaphoreType.DMA((n * cap,)) for n in (n_in, n_out)]
+
+    to_next, tab = pl.pallas_call(
         functools.partial(send_kernel, cap, sectors, sec_count),
-        out_shape=[wire, wire, jax.ShapeDtypeStruct((4 * slots,), jnp.int32)],
+        out_shape=[wire, jax.ShapeDtypeStruct((6 * slots,), jnp.int32)],
         in_specs=[SMEM, SMEM, SMEM, ANY],
-        out_specs=[ANY, ANY, SMEM],
-        scratch_shapes=[
-            pltpu.VMEM((2 * cap,) + raw_slot, BF16),
-            pltpu.VMEM((2 * cap,) + share, BF16),
-            pltpu.SemaphoreType.DMA((2 * cap,)),
-            pltpu.SemaphoreType.DMA((2 * cap,)),
-        ]
-        + flats,
+        out_specs=[ANY, SMEM],
+        scratch_shapes=gather(1, 1) + semaphores(1, 1) + flats,
         name="send",
-    )(*listing, displacement)
+    )(sec, pair_list.T, pair_count, displacement)
 
     forward = [(i, (i + 1) % sec_count) for i in range(sec_count)]
     backward = [((i + 1) % sec_count, i) for i in range(sec_count)]
     from_prev = lax.ppermute(to_next, "sec", forward)
-
-    def gather(n):
-        return [
-            pltpu.VMEM((2 * cap,) + raw_slot, BF16),
-            pltpu.VMEM((n * cap,) + share, BF16),
-        ]
 
     diff_local = pl.pallas_call(
         functools.partial(local_kernel, cap),
         out_shape=wire,
         in_specs=[SMEM, ANY],
         out_specs=ANY,
-        scratch_shapes=gather(1)
-        + [pltpu.SemaphoreType.DMA((2 * cap,)), pltpu.SemaphoreType.DMA((cap,))]
-        + flats,
+        scratch_shapes=gather(2, 1) + semaphores(2, 1) + flats,
         name="local",
-    )(own, displacement)
+    )(tab, displacement)
     limit = contact_limit.reshape(-1)
     limit = jnp.concatenate([limit, 1.0 / limit])
-    gathered = pl.pallas_call(
-        functools.partial(partner_kernel, cap, sectors, sec_count, calls),
-        out_shape=[wire] * 2
-        + [jax.ShapeDtypeStruct((6 * n,), jnp.int32) for n in (slots, cap)]
+    at_a, to_prev, at_b, lead, limits = pl.pallas_call(
+        functools.partial(partner_kernel, cap, sectors, calls),
+        out_shape=[wire] * 3
+        + [jax.ShapeDtypeStruct((6 * cap,), jnp.int32)]
         + [jax.ShapeDtypeStruct((2 * slots * contact_limit.shape[2],), F32)],
-        in_specs=[SMEM] * 5 + [ANY, ANY],
-        out_specs=[ANY, ANY, SMEM, SMEM, SMEM],
-        scratch_shapes=gather(2)
+        in_specs=[SMEM, SMEM, ANY, ANY],
+        out_specs=[ANY, ANY, ANY, SMEM, SMEM],
+        scratch_shapes=gather(3, 3)
         + [pltpu.SMEM((sectors * blocks,), jnp.int32)]
-        + [pltpu.SemaphoreType.DMA((2 * cap,))] * 2
+        + semaphores(3, 3)
         + flats,
         name="partner",
-    )(*listing, own, limit, displacement, diff_local)
-    at_a, at_b, tab, lead, limits = gathered
-
-    to_prev, from_prev, at_b = lax.optimization_barrier((to_prev, from_prev, at_b))
+    )(tab, limit, displacement, diff_local)
+    to_prev, from_prev = lax.optimization_barrier((to_prev, from_prev))
     from_next = lax.ppermute(to_prev, "sec", backward)
-
 
     def exchange(x):
         return lax.all_to_all(x, "harm", split_axis=0, concat_axis=0, tiled=True)
@@ -607,14 +555,9 @@
         return pl.pallas_call(
             functools.partial(friction_kernel, cap, group, first, bool(extra)),
             out_shape=double if extra else wire,
-            in_specs=[SMEM, VMEM, VMEM] + [ANY] * (1 + len(extra)),
+            in_specs=[SMEM] + [VMEM] * (3 + len(extra)),
             out_specs=ANY,
-            scratch_shapes=[
-                pltpu.VMEM((cap,) + share, BF16),
-                pltpu.VMEM((n,) + share, BF16),
-                pltpu.SemaphoreType.DMA((4, n)),
-            ]
-            + [pltpu.VMEM((cap,) + share, BF16)] * len(extra),
+            scratch_shapes=[pltpu.VMEM((n,) + share, BF16), pltpu.SemaphoreType.DMA((n,))],
             compiler_params=memory(12),
             name="friction",
         )(limits, fwd, inv, x, *extra)

time: 120 us -> 118 us (0.983)
  Pallas kernels: 59.9 us -> 57 us
  waiting for transfers between devices: 17.6 us -> 19.5 us
    pallas_call x3, Pallas kernels: 9.73 us -> 8.4 us  [friction(): pl.pallas_call(functools.partial(friction_kernel, cap, group, first, bool...]
  transfers between devices with their start and end apart: 8 -> 8, of which waited for: 6 -> 6; matrix products, arithmetic and copies ran while one was open for 1% -> 2% of each run, Pallas kernels for 38% -> 37%
where the time goes in v2:
time: 118 us; the launch traced here: 117 us
  Pallas kernels  57 us (48%)
  starting transfers between devices  21.8 us (18%)
  waiting for transfers between devices  19.5 us (17%)
  blocking collectives  13.5 us (11%)
  local copies, waits for them, and re-layouts  4.6 us (4%)
    pallas_call x3, Pallas kernels, stiffness_product(): pl.pallas_call(functools.partial(stiffness_kernel, len(extra)), grid=(cou...  27.1 us
    all_to_all x4, starting transfers between devices, exchange(): return lax.all_to_all(x, 'harm', split_axis=0, concat_axis=0, tiled=True)  15 us
    all_to_all x1, blocking collectives, exchange(): return lax.all_to_all(x, 'harm', split_axis=0, concat_axis=0, tiled=True)  13.5 us
    all_to_all x4, waiting for transfers between devices, exchange(): return lax.all_to_all(x, 'harm', split_axis=0, concat_axis=0, tiled=True)  10.3 us
    pallas_call x3, Pallas kernels, friction(): pl.pallas_call(functools.partial(friction_kernel, cap, group, first, bool...  8.4 us
    pallas_call x2, Pallas kernels, add_pairs(): pl.pallas_call(functools.partial(add_kernel, cap, specs, start, len(deps)...  7.52 us
    pallas_call x1, Pallas kernels, on_device(): pl.pallas_call(functools.partial(partner_kernel, cap, sectors, calls), ou...  5.76 us
    ppermute x1, waiting for transfers between devices, on_device(): ret_b = lax.ppermute(back_b, 'sec', forward)  5.38 us
  transfers between devices with their start and end apart: 8, of which 6 were waited for; matrix products, arithmetic and copies ran while one was open for 2% of the time, Pallas kernels for 37%

profile of v2, /device:TPU:0, one launch (start us, length us, event | category | flops | bytes accessed | tf_op | source)
XLA Modules:
  0.0 117.3 jit_solution(6213638906549095054)
XLA Ops:
  0.0 4.6 %send.1 = (bf16[8,6,48,128]{3,2,1,0:T(8,128)(2,1)}, s32[108]{0:T(128)}) custom-call(s32[1]{0:T(128)} %bitcast.sec_ref, s32[3,72]{1,0:T(4,128)} %bitcast.8, s32[4]{0:T(128)} %count_ref.1, bf16[3,8,32,48,128]{4,3,2,1,0:T(8,128)(2,1)} %disp_ref.5), custom_call_target="tpu_custom_call" | custom-call | tf_op jit(solution)/shard_map/send/pallas_call | solution.py:508
  4.6 3.1 %collective-permute-start = (bf16[8,6,48,128]{3,2,1,0:T(8,128)(2,1)}, bf16[8,6,48,128]{3,2,1,0:T(8,128)(2,1)S(1)}, u32[]{:S(2)}, u32[]{:S(2)}) collective-permute-start(bf16[8,6,48,128]{3,2,1,0:T(8,128)(2,1)} %get-tuple-element.21), channel_id=1, source_target_pairs={{0,8},{8,16},{16,24},{24,0},{1,9},{9,17},{17,25},{25,1},{2,10},{10... | collective-permute-start | bytes 1769480 | tf_op jit(solution)/shard_map/ppermute | solution.py:519
  7.7 3.5 %local.1.dep_ref = bf16[8,6,48,128]{3,2,1,0:T(8,128)(2,1)} custom-call(s32[108]{0:T(128)} %get-tuple-element.17.tab_ref, bf16[3,8,32,48,128]{4,3,2,1,0:T(8,128)(2,1)} %disp_ref.5), custom_call_target="tpu_custom_call" | custom-call | tf_op jit(solution)/shard_map/local/pallas_call | solution.py:521
  11.2 3.7 %all-to-all-start = ((bf16[8,6,48,128]{3,2,1,0:T(8,128)(2,1)}), bf16[8,6,48,128]{3,2,1,0:T(8,128)(2,1)S(1)}, u32[]{:S(2)}, u32[]{:S(2)}) async-start(bf16[8,6,48,128]{3,2,1,0:T(8,128)(2,1)} %local.1.dep_ref), calls=%async_computation | async-start | bytes 1179648 | tf_op jit(solution)/shard_map/all_to_all | solution.py:548
  15.9 5.8 %partner.1 = (bf16[8,6,48,128]{3,2,1,0:T(8,128)(2,1)}, bf16[8,6,48,128]{3,2,1,0:T(8,128)(2,1)}, bf16[8,6,48,128]{3,2,1,0:T(8,128)(2,1)}, s32[36]{0:T(128)}, f32[216]{0:T(256)}) custom-call(s32[108]{0:T(128)} %get-tuple-element.17.tab_ref, f32[1152]{0:T(1024)} %pad_maximum_fusion.lim_ref, bf16[3,8,32,48,128]{4,3,2,1,0:T(8,128)(2,1)} %disp_ref.5, ...), custom_call_target="tpu_custom_call" | custom-call | tf_op jit(solution)/shard_map/partner/pallas_call | solution.py:531
  21.7 1.6 %collective-permute-done.x_ref = bf16[8,6,48,128]{3,2,1,0:T(8,128)(2,1)S(1)} collective-permute-done((bf16[8,6,48,128]{3,2,1,0:T(8,128)(2,1)}, bf16[8,6,48,128]{3,2,1,0:T(8,128)(2,1)S(1)}, u32[]{:S(2)}, u32[]{:S(2)}) %collective-permute-start) | collective-permute-done | bytes 589856 | tf_op jit(solution)/shard_map/ppermute | solution.py:519
  23.2 1.7 %collective-permute-start.1 = (bf16[8,6,48,128]{3,2,1,0:T(8,128)(2,1)}, bf16[8,6,48,128]{3,2,1,0:T(8,128)(2,1)S(1)}, u32[]{:S(2)}, u32[]{:S(2)}) collective-permute-start(bf16[8,6,48,128]{3,2,1,0:T(8,128)(2,1)} %get-tuple-element.24), channel_id=1, source_target_pairs={{8,0},{16,8},{24,16},{0,24},{9,1},{17,9},{25,17},{1,25},{10,2},{18... | collective-permute-start | bytes 1769480 | tf_op jit(solution)/shard_map/ppermute | solution.py:545
  26.6 13.5 %all_to_all.25.x_ref = bf16[8,6,48,128]{3,2,1,0:T(8,128)(2,1)S(1)} all-to-all(bf16[8,6,48,128]{3,2,1,0:T(8,128)(2,1)S(1)} %difference.1.refs_0_), channel_id=1, replica_groups=mesh['sec'=4,'harm'=8] {'harm'}, dimensions={0} | all-to-all | bytes 1179648 | tf_op jit(solution)/shard_map/all_to_all | solution.py:548
  41.9 3.0 %friction.3.refs_1_ = bf16[8,12,48,128]{3,2,1,0:T(8,128)(2,1)} custom-call(f32[216]{0:T(256)S(1)} %copy-done.5, bf16[128,64]{1,0:T(8,128)(2,1)S(1)} %copy-done.3, bf16[64,128]{1,0:T(8,128)(2,1)S(1)} %copy-done.4, bf16[8,6,48,128]{3,2,1,0:T(8,128)(2,1)S(1)} %all_to_all.25.x_ref, bf16[8,6,48,128]{3,2,1,0:T(8,128)(2,1)S(1)} %collective-permute-done.1.refs_0_, ...), custom_call_target="tpu_custom_call" | custom-call | tf_op jit(solution)/shard_map/friction/pallas_call | solution.py:555
  44.9 3.6 %all-to-all-start.2 = ((bf16[8,12,48,128]{3,2,1,0:T(8,128)(2,1)}), bf16[8,12,48,128]{3,2,1,0:T(8,128)(2,1)S(1)}, u32[]{:S(2)}, u32[]{:S(2)}) async-start(bf16[8,12,48,128]{3,2,1,0:T(8,128)(2,1)} %friction.3.refs_1_), calls=%async_computation.2 | async-start | bytes 2359296 | tf_op jit(solution)/shard_map/all_to_all | solution.py:548
  49.1 2.7 %friction.5 = bf16[8,6,48,128]{3,2,1,0:T(8,128)(2,1)} custom-call(f32[216]{0:T(256)S(1)} %copy-done.6, bf16[128,64]{1,0:T(8,128)(2,1)S(1)} %copy-done.3, bf16[64,128]{1,0:T(8,128)(2,1)S(1)} %copy-done.4, bf16[8,6,48,128]{3,2,1,0:T(8,128)(2,1)S(1)} %all-to-all-done.refs_0_.x_ref), custom_call_target="tpu_custom_call" | custom-call | tf_op jit(solution)/shard_map/friction/pallas_call | solution.py:555
  51.9 7.4 %stiffness_product.3.refs_0_ = bf16[3,4,2,1536,128]{4,3,2,1,0:T(8,128)(2,1)} custom-call(bf16[4,1536,1536]{2,1,0:T(8,128)(2,1)} %matrix_ref.5, bf16[3,4,2,1536,128]{4,3,2,1,0:T(8,128)(2,1)} %bitcast.4, bf16[8,6,48,128]{3,2,1,0:T(8,128)(2,1)} %copy-done), custom_call_target="tpu_custom_call" | custom-call | flops 3623878656 | bytes 9437184 | tf_op jit(solution)/shard_map/stiffness_product/pallas_call | solution.py:455
  59.3 5.9 %all-to-all-done.2.x_ref.refs_0_ = bf16[8,12,48,128]{3,2,1,0:T(8,128)(2,1)S(1)} async-done(((bf16[8,12,48,128]{3,2,1,0:T(8,128)(2,1)}), bf16[8,12,48,128]{3,2,1,0:T(8,128)(2,1)S(1)}, u32[]{:S(2)}, u32[]{:S(2)}) %all-to-all-start.2) | async-done | bytes 1179680 | tf_op jit(solution)/shard_map/all_to_all | solution.py:548
  65.2 2.7 %friction.4.refs_1_ = bf16[8,6,48,128]{3,2,1,0:T(8,128)(2,1)} custom-call(f32[216]{0:T(256)S(1)} %copy-done.6, bf16[128,64]{1,0:T(8,128)(2,1)S(1)} %copy-done.3, bf16[64,128]{1,0:T(8,128)(2,1)S(1)} %copy-done.4, bf16[8,12,48,128]{3,2,1,0:T(8,128)(2,1)S(1)} %all-to-all-done.2.x_ref.refs_0_), custom_call_target="tpu_custom_call" | custom-call | tf_op jit(solution)/shard_map/friction/pallas_call | solution.py:555
  67.9 3.5 %all-to-all-start.3 = ((bf16[8,6,48,128]{3,2,1,0:T(8,128)(2,1)}), bf16[8,6,48,128]{3,2,1,0:T(8,128)(2,1)S(1)}, u32[]{:S(2)}, u32[]{:S(2)}) async-start(bf16[8,6,48,128]{3,2,1,0:T(8,128)(2,1)} %friction.4.refs_1_), calls=%async_computation.3 | async-start | bytes 1179648 | tf_op jit(solution)/shard_map/all_to_all | solution.py:548
  71.5 12.3 %stiffness_product.4.refs_0_ = bf16[3,4,2,1536,128]{4,3,2,1,0:T(8,128)(2,1)} custom-call(bf16[4,1536,1536]{2,1,0:T(8,128)(2,1)} %matrix_ref.5, bf16[3,4,2,1536,128]{4,3,2,1,0:T(8,128)(2,1)} %bitcast.5, bf16[3,4,2,1536,128]{4,3,2,1,0:T(8,128)(2,1)} %stiffness_product.3.refs_0_, bf16[8,12,48,128]{3,2,1,0:T(8,128)(2,1)} %friction.3.refs_1_), custom_call_target="tpu_custom_call", output_to_operand_aliasing={{}: (2, {})} | custom-call | flops 7247757312 | bytes 18874368 | tf_op jit(solution)/shard_map/stiffness_product/pallas_call | solution.py:455
  84.6 1.5 %collective-permute-start.3 = (bf16[8,6,48,128]{3,2,1,0:T(8,128)(2,1)}, bf16[8,6,48,128]{3,2,1,0:T(8,128)(2,1)S(1)}, u32[]{:S(2)}, u32[]{:S(2)}) collective-permute-start(bf16[8,6,48,128]{3,2,1,0:T(8,128)(2,1)} %slice.4), channel_id=1, source_target_pairs={{8,0},{16,8},{24,16},{0,24},{9,1},{17,9},{25,17},{1,25},{10,2},{18... | collective-permute-start | bytes 1769480 | tf_op jit(solution)/shard_map/ppermute | solution.py:584
  86.2 7.4 %stiffness_product.5 = bf16[3,4,2,1536,128]{4,3,2,1,0:T(8,128)(2,1)} custom-call(bf16[4,1536,1536]{2,1,0:T(8,128)(2,1)} %matrix_ref.5, bf16[3,4,2,1536,128]{4,3,2,1,0:T(8,128)(2,1)} %bitcast.6, bf16[3,4,2,1536,128]{4,3,2,1,0:T(8,128)(2,1)} %stiffness_product.4.refs_0_, bf16[8,6,48,128]{3,2,1,0:T(8,128)(2,1)} %friction.4.refs_1_), custom_call_target="tpu_custom_call", output_to_operand_aliasing={{}: (2, {})} | custom-call | flops 3623878656 | bytes 9437184 | tf_op jit(solution)/shard_map/stiffness_product/pallas_call | solution.py:455
  94.1 4.1 %all-to-all-start.4 = ((bf16[8,6,48,128]{3,2,1,0:T(8,128)(2,1)}), bf16[8,6,48,128]{3,2,1,0:T(8,128)(2,1)S(1)}, u32[]{:S(2)}, u32[]{:S(2)}) async-start(bf16[8,6,48,128]{3,2,1,0:T(8,128)(2,1)} %friction.5), calls=%async_computation.4 | async-start | bytes 1179648 | tf_op jit(solution)/shard_map/all_to_all | solution.py:548
  98.2 2.3 %collective-permute-done.3.refs_2_ = bf16[8,6,48,128]{3,2,1,0:T(8,128)(2,1)S(1)} collective-permute-done((bf16[8,6,48,128]{3,2,1,0:T(8,128)(2,1)}, bf16[8,6,48,128]{3,2,1,0:T(8,128)(2,1)S(1)}, u32[]{:S(2)}, u32[]{:S(2)}) %collective-permute-start.3) | collective-permute-done | bytes 589856 | tf_op jit(solution)/shard_map/ppermute | solution.py:584
  100.5 4.2 %add_pairs.2.refs_2_ = bf16[3,8,32,48,128]{4,3,2,1,0:T(8,128)(2,1)} custom-call(s32[108]{0:T(128)S(1)} %copy-done.7, s32[36]{0:T(128)S(1)} %copy-done.8, bf16[8,12,48,128]{3,2,1,0:T(8,128)(2,1)S(1)} %all-to-all-done.2.x_ref.refs_0_, bf16[8,6,48,128]{3,2,1,0:T(8,128)(2,1)S(1)} %all-to-all-done.3.refs_1_, ...), custom_call_target="tpu_custom_call", output_to_operand_aliasing={{}: (5, {})} | custom-call | tf_op jit(solution)/shard_map/add_pairs/pallas_call | solution.py:422
  104.6 3.9 %all-to-all-done.4.refs_0_ = bf16[8,6,48,128]{3,2,1,0:T(8,128)(2,1)S(1)} async-done(((bf16[8,6,48,128]{3,2,1,0:T(8,128)(2,1)}), bf16[8,6,48,128]{3,2,1,0:T(8,128)(2,1)S(1)}, u32[]{:S(2)}, u32[]{:S(2)}) %all-to-all-start.4) | async-done | bytes 589856 | tf_op jit(solution)/shard_map/all_to_all | solution.py:548
  108.6 5.4 %collective-permute-done.2.refs_1_ = bf16[8,6,48,128]{3,2,1,0:T(8,128)(2,1)S(1)} collective-permute-done((bf16[8,6,48,128]{3,2,1,0:T(8,128)(2,1)S(1)}, bf16[8,6,48,128]{3,2,1,0:T(8,128)(2,1)S(1)}, u32[]{:S(2)}, u32[]{:S(2)}) %collective-permute-start.2) | collective-permute-done | bytes 589856 | tf_op jit(solution)/shard_map/ppermute | solution.py:589
  114.0 3.3 %add_pairs.3 = bf16[3,8,32,48,128]{4,3,2,1,0:T(8,128)(2,1)} custom-call(s32[108]{0:T(128)S(1)} %copy-done.7, s32[36]{0:T(128)S(1)} %copy-done.8, bf16[8,6,48,128]{3,2,1,0:T(8,128)(2,1)S(1)} %all-to-all-done.4.refs_0_, bf16[8,6,48,128]{3,2,1,0:T(8,128)(2,1)S(1)} %collective-permute-done.2.refs_1_, ...), custom_call_target="tpu_custom_call", output_to_operand_aliasing={{}: (4, {})} | custom-call | tf_op jit(solution)/shard_map/add_pairs/pallas_call | solution.py:422
  (30 shorter events, 6.4 us)
Async XLA Ops:
  0.0 15.0 %copy-start.9 = (f32[3,32,6]{1,2,0:T(8,128)S(1)}, f32[3,32,6]{1,2,0:T(8,128)}, u32[]{:S(2)}) copy-start(f32[3,32,6]{1,2,0:T(8,128)} %param.9) | copy-start | bytes 6916
  4.6 18.7 %collective-permute-start = (bf16[8,6,48,128]{3,2,1,0:T(8,128)(2,1)}, bf16[8,6,48,128]{3,2,1,0:T(8,128)(2,1)S(1)}, u32[]{:S(2)}, u32[]{:S(2)}) collective-permute-start(bf16[8,6,48,128]{3,2,1,0:T(8,128)(2,1)} %get-tuple-element.21), channel_id=1, source_target_pairs={{0,8},{8,16},{16,24},{24,0},{1,9},{9,17},{17,25},{25,1},{2,10},{10... | collective-permute-start | bytes 1769480 | tf_op jit(solution)/shard_map/ppermute | solution.py:519
  11.2 28.9 %copy-start.3 = (bf16[128,64]{1,0:T(8,128)(2,1)S(1)}, bf16[128,64]{1,0:T(8,128)(2,1)}, u32[]{:S(2)}) copy-start(bf16[128,64]{1,0:T(8,128)(2,1)} %constant.11.clone.fwd_ref) | copy-start | bytes 49156
  11.2 28.9 %copy-start.4 = (bf16[64,128]{1,0:T(8,128)(2,1)S(1)}, bf16[64,128]{1,0:T(8,128)(2,1)}, u32[]{:S(2)}) copy-start(bf16[64,128]{1,0:T(8,128)(2,1)} %constant.12.clone.inv_ref) | copy-start | bytes 49156
  11.2 14.1 %all-to-all-start = ((bf16[8,6,48,128]{3,2,1,0:T(8,128)(2,1)}), bf16[8,6,48,128]{3,2,1,0:T(8,128)(2,1)S(1)}, u32[]{:S(2)}, u32[]{:S(2)}) async-start(bf16[8,6,48,128]{3,2,1,0:T(8,128)(2,1)} %local.1.dep_ref), calls=%async_computation | async-start | bytes 1179648 | tf_op jit(solution)/shard_map/all_to_all | solution.py:548
  23.2 16.9 %collective-permute-start.1 = (bf16[8,6,48,128]{3,2,1,0:T(8,128)(2,1)}, bf16[8,6,48,128]{3,2,1,0:T(8,128)(2,1)S(1)}, u32[]{:S(2)}, u32[]{:S(2)}) collective-permute-start(bf16[8,6,48,128]{3,2,1,0:T(8,128)(2,1)} %get-tuple-element.24), channel_id=1, source_target_pairs={{8,0},{16,8},{24,16},{0,24},{9,1},{17,9},{25,17},{1,25},{10,2},{18... | collective-permute-start | bytes 1769480 | tf_op jit(solution)/shard_map/ppermute | solution.py:545
  25.4 1.1 copy-start.2
  26.6 25.2 %copy-start = (bf16[8,6,48,128]{3,2,1,0:T(8,128)(2,1)}, bf16[8,6,48,128]{3,2,1,0:T(8,128)(2,1)S(1)}, u32[]{:S(2)}) copy-start(bf16[8,6,48,128]{3,2,1,0:T(8,128)(2,1)S(1)} %difference.1.refs_0_) | copy-start | bytes 1769476
  40.2 1.1 copy-start.1
  41.2 0.7 copy-start.5
  44.9 20.3 %all-to-all-start.2 = ((bf16[8,12,48,128]{3,2,1,0:T(8,128)(2,1)}), bf16[8,12,48,128]{3,2,1,0:T(8,128)(2,1)S(1)}, u32[]{:S(2)}, u32[]{:S(2)}) async-start(bf16[8,12,48,128]{3,2,1,0:T(8,128)(2,1)} %friction.3.refs_1_), calls=%async_computation.2 | async-start | bytes 2359296 | tf_op jit(solution)/shard_map/all_to_all | solution.py:548
  48.5 0.7 copy-start.6
  67.9 25.6 %all-to-all-start.3 = ((bf16[8,6,48,128]{3,2,1,0:T(8,128)(2,1)}), bf16[8,6,48,128]{3,2,1,0:T(8,128)(2,1)S(1)}, u32[]{:S(2)}, u32[]{:S(2)}) async-start(bf16[8,6,48,128]{3,2,1,0:T(8,128)(2,1)} %friction.4.refs_1_), calls=%async_computation.3 | async-start | bytes 1179648 | tf_op jit(solution)/shard_map/all_to_all | solution.py:548
  84.6 15.8 %copy-start.7 = (s32[108]{0:T(128)S(1)}, s32[108]{0:T(128)}, u32[]{:S(2)}) copy-start(s32[108]{0:T(128)} %get-tuple-element.17.tab_ref) | copy-start | bytes 1300
  84.6 15.8 %copy-start.8 = (s32[36]{0:T(128)S(1)}, s32[36]{0:T(128)}, u32[]{:S(2)}) copy-start(s32[36]{0:T(128)} %get-tuple-element.18.lead_ref) | copy-start | bytes 436
  84.6 15.8 %collective-permute-start.3 = (bf16[8,6,48,128]{3,2,1,0:T(8,128)(2,1)}, bf16[8,6,48,128]{3,2,1,0:T(8,128)(2,1)S(1)}, u32[]{:S(2)}, u32[]{:S(2)}) collective-permute-start(bf16[8,6,48,128]{3,2,1,0:T(8,128)(2,1)} %slice.4), channel_id=1, source_target_pairs={{8,0},{16,8},{24,16},{0,24},{9,1},{17,9},{25,17},{1,25},{10,2},{18... | collective-permute-start | bytes 1769480 | tf_op jit(solution)/shard_map/ppermute | solution.py:584
  93.6 20.4 %collective-permute-start.2 = (bf16[8,6,48,128]{3,2,1,0:T(8,128)(2,1)S(1)}, bf16[8,6,48,128]{3,2,1,0:T(8,128)(2,1)S(1)}, u32[]{:S(2)}, u32[]{:S(2)}) collective-permute-start(bf16[8,6,48,128]{3,2,1,0:T(8,128)(2,1)S(1)} %all-to-all-done.3.refs_1_), channel_id=1, source_target_pairs={{0,8},{8,16},{16,24},{24,0},{1,9},{9,17},{17,25},{25,1},{2,10},{10... | collective-permute-start | bytes 1769480 | tf_op jit(solution)/shard_map/ppermute | solution.py:589
  94.1 14.5 %all-to-all-start.4 = ((bf16[8,6,48,128]{3,2,1,0:T(8,128)(2,1)}), bf16[8,6,48,128]{3,2,1,0:T(8,128)(2,1)S(1)}, u32[]{:S(2)}, u32[]{:S(2)}) async-start(bf16[8,6,48,128]{3,2,1,0:T(8,128)(2,1)} %friction.5), calls=%async_computation.4 | async-start | bytes 1179648 | tf_op jit(solution)/shard_map/all_to_all | solution.py:548
